TPU v7x, 32 devices: a whole 2x2x4 slice. The times are simulated.
32 devices in a mesh: replica: 8 (over y, x, core), shard: 4 (over z).
Axes of the slice: x: 2, y: 2, z: 4, core: 2. Of those that a mesh axis runs over, the one named last changes fastest.
Arguments:
- inputs: float32 [64, 512, 1024], P(('replica', 'shard')), may hold values from -6 to 6
- lengths: int32 [64], P(('replica', 'shard')), may hold values from 1 to 512, 24576 in all
- cotangent: float32 [64, 512, 1024], P(('replica', 'shard')), may hold values from -6 to 6
- w_in: bfloat16 [2, 1024, 4384], P(None, 'shard'), may hold values from -0.1875 to 0.1875
- w_out: bfloat16 [2, 2048, 1024], P(None, 'shard'), may hold values from -0.125 to 0.125
- norm_gain: float32 [2, 1024], replicated, may hold values from 0.5 to 1.5
- conv_weight: float32 [2, 4, 2304], replicated, may hold values from -3 to 3
- conv_bias: float32 [2, 2304], replicated, may hold values from -3 to 3
- gate_gain: float32 [2, 2048], replicated, may hold values from 0.5 to 1.5
- dt_bias: float32 [2, 32], replicated, may hold values from -6.9 to -2.3
- a_log: float32 [2, 32], replicated, may hold values from 0 to 2.77
- skip: float32 [2, 32], replicated, may hold values from 0.5 to 1.5
Outputs:
- output: float32 [64, 512, 1024], P(('replica', 'shard'))
- input_grad: float32 [64, 512, 1024], P(('replica', 'shard'))
- grad_w_in: float32 [2, 1024, 4384], P(None, 'shard')
- grad_w_out: float32 [2, 2048, 1024], P(None, 'shard')
- grad_norm_gain: float32 [2, 1024], replicated
- grad_conv_weight: float32 [2, 4, 2304], replicated
- grad_conv_bias: float32 [2, 2304], replicated
- grad_gate_gain: float32 [2, 2048], replicated
- grad_dt_bias: float32 [2, 32], replicated
- grad_a_log: float32 [2, 32], replicated
- grad_skip: float32 [2, 32], replicated
Inputs may be any that keep to these rules, and one draw needn't show every extreme that they name: `lengths`: every sequence has at least one token; the longest in each draw has exactly 512.
All inputs are finite; a program needn't handle non-finite values. No bound on the sum of `lengths` on one device may be relied on, other than what follows from the above.
Results may differ from a plain program's by a relative error of at most 0.028.
Values may be sent and summed in bfloat16 or wider, within the bound.
No kernel may reach another device: no remote copies, remote signals or barrier semaphores. Data moves between devices by JAX's collectives and lax.ppermute only.
A program may use at most 320 MiB of HBM per device.

v0:
```python
import jax
import jax.numpy as jnp
from jax import lax
from jax.sharding import PartitionSpec as P

DI = 2048
HEADS = 32
HEAD_DIM = 64
STATE = 128
CONV = 4
SPAN = 256
LEN = 512


EPSILON = 1e-05
HIGHEST = lax.Precision.HIGHEST


def rms_scale(values, gain):
    return values * lax.rsqrt(jnp.mean(values * values, axis=-1, keepdims=True) + EPSILON) * gain


def span_scan(inner_x, step_size, rate, b_input, c_output):
    seq_len = inner_x.shape[0]
    blocks = seq_len // SPAN
    logs = (step_size * rate[None, :]).reshape(blocks, SPAN, HEADS)
    cum_logs = jnp.cumsum(logs, axis=1)
    scaled_x = (inner_x * step_size[:, :, None]).reshape(blocks, SPAN, HEADS, HEAD_DIM)
    b_blocks = b_input.reshape(blocks, SPAN, STATE)
    c_blocks = c_output.reshape(blocks, SPAN, STATE)
    scores = jnp.einsum("cqn,ckn->cqk", c_blocks, b_blocks, precision=HIGHEST)
    row_index = lax.broadcasted_iota(jnp.int32, (SPAN, SPAN), 0)
    col_index = lax.broadcasted_iota(jnp.int32, (SPAN, SPAN), 1)
    causal = (row_index >= col_index)[None, None, :, :]
    cum_heads = jnp.transpose(cum_logs, (0, 2, 1))
    log_gaps = cum_heads[:, :, :, None] - cum_heads[:, :, None, :]
    decays = jnp.where(causal, jnp.exp(jnp.where(causal, log_gaps, 0.0)), 0.0)
    mixing = decays * scores[:, None, :, :]
    intra = jnp.einsum("chqk,ckhp->cqhp", mixing, scaled_x, precision=HIGHEST)
    to_end = jnp.exp(cum_logs[:, -1:, :] - cum_logs)
    states = jnp.einsum(
        "ckhp,ckn->chpn", scaled_x * to_end[:, :, :, None], b_blocks, precision=HIGHEST
    )
    totals = jnp.exp(cum_logs[:, -1, :])
    carried = jnp.zeros((HEADS, HEAD_DIM, STATE), jnp.float32)
    previous = []
    for block in range(blocks):
        previous.append(carried)
        carried = totals[block][:, None, None] * carried + states[block]
    previous = jnp.stack(previous)
    inter = (
        jnp.einsum("cqn,chpn->cqhp", c_blocks, previous, precision=HIGHEST)
        * jnp.exp(cum_logs)[:, :, :, None]
    )
    return (intra + inter).reshape(seq_len, HEADS, HEAD_DIM)


def mix_one(projected, conv_weight, conv_bias, gate_gain, dt_bias, a_log, skip):
    seq_len = projected.shape[0]
    gate_part = projected[:, :DI]
    conv_in = projected[:, DI : 2 * DI + 2 * STATE]
    raw_step = projected[:, 2 * DI + 2 * STATE :]
    padded = jnp.pad(conv_in, ((CONV - 1, 0), (0, 0)))
    pre_act = conv_bias[None, :] + conv_weight[0][None, :] * padded[0:seq_len]
    for offset in range(1, CONV):
        pre_act = pre_act + conv_weight[offset][None, :] * padded[offset : offset + seq_len]
    act = jax.nn.silu(pre_act)
    inner_x = act[:, :DI].reshape(seq_len, HEADS, HEAD_DIM)
    b_input = act[:, DI : DI + STATE]
    c_output = act[:, DI + STATE :]
    step_size = jax.nn.softplus(raw_step + dt_bias[None, :])
    scanned = span_scan(inner_x, step_size, -jnp.exp(a_log), b_input, c_output)
    scanned = scanned + skip[None, :, None] * inner_x
    gated = scanned.reshape(seq_len, DI) * jax.nn.silu(gate_part)
    return rms_scale(gated, gate_gain)


def mix_part(projected, extras):
    by_seq = projected.reshape(-1, LEN, projected.shape[1])
    one_seq = jax.checkpoint(lambda row: mix_one(row, *extras))
    return lax.map(one_seq, by_seq).reshape(projected.shape[0], DI)


def contract_rows(left, right):
    return lax.dot_general(
        left, right, (((0,), (0,)), ((), ())), preferred_element_type=jnp.float32
    )


def contract_cols(left, right):
    return lax.dot_general(
        left, right, (((1,), (1,)), ((), ())), preferred_element_type=jnp.float32
    )


def per_device(
    inputs,
    lengths,
    cotangent,
    w_in,
    w_out,
    norm_gain,
    conv_weight,
    conv_bias,
    gate_gain,
    dt_bias,
    a_log,
    skip,
):
    slot_count, seq_len, width = inputs.shape
    row_total = slot_count * seq_len
    places = lax.broadcasted_iota(jnp.int32, (slot_count, seq_len), 1)
    valid_mask = (places < lengths[:, None]).astype(jnp.float32).reshape(row_total, 1)
    layer_count = w_in.shape[0]
    hidden = inputs.reshape(row_total, width)
    saved = []
    for layer in range(layer_count):
        full_in, full_out = (
            lax.all_gather(w_in[layer], "shard", axis=0, tiled=True),
            lax.all_gather(w_out[layer], "shard", axis=0, tiled=True),
        )
        extras = (
            conv_weight[layer],
            conv_bias[layer],
            gate_gain[layer],
            dt_bias[layer],
            a_log[layer],
            skip[layer],
        )
        normed_full, norm_pull = jax.vjp(rms_scale, hidden, norm_gain[layer])
        normed = normed_full.astype(jnp.bfloat16)
        projected = jnp.dot(normed, full_in, preferred_element_type=jnp.float32)
        mixed_full, mix_pull = jax.vjp(mix_part, projected, extras)
        mixed = mixed_full.astype(jnp.bfloat16)
        branch = jnp.dot(mixed, full_out, preferred_element_type=jnp.float32)
        hidden = hidden + valid_mask * branch
        saved.append((normed, mixed, norm_pull, mix_pull, None, None))
    grad_stream = cotangent.reshape(row_total, width)
    in_parts = [None] * layer_count
    out_parts = [None] * layer_count
    gain_parts = [None] * layer_count
    extra_parts = [None] * layer_count
    for layer in reversed(range(layer_count)):
        normed, mixed, norm_pull, mix_pull, full_in, full_out = saved[layer]
        full_in, full_out = (
            lax.all_gather(w_in[layer], "shard", axis=0, tiled=True),
            lax.all_gather(w_out[layer], "shard", axis=0, tiled=True),
        )
        d_branch = (valid_mask * grad_stream).astype(jnp.bfloat16)
        local_out = contract_rows(mixed, d_branch)
        d_mixed = contract_cols(d_branch, full_out)
        d_projected, d_extras = mix_pull(d_mixed)
        d_proj_low = d_projected.astype(jnp.bfloat16)
        local_in = contract_rows(normed, d_proj_low)
        d_normed = contract_cols(d_proj_low, full_in)
        d_hidden, d_gain = norm_pull(d_normed)
        grad_stream = grad_stream + d_hidden
        owned_in, owned_out = (
            lax.psum_scatter(
                local_in.astype(jnp.bfloat16), "shard", scatter_dimension=0, tiled=True
            ).astype(jnp.float32),
            lax.psum_scatter(
                local_out.astype(jnp.bfloat16), "shard", scatter_dimension=0, tiled=True
            ).astype(jnp.float32),
        )
        owned_in, owned_out = (
            lax.psum(owned_in.astype(jnp.bfloat16), "replica").astype(jnp.float32),
            lax.psum(owned_out.astype(jnp.bfloat16), "replica").astype(jnp.float32),
        )
        in_parts[layer] = owned_in
        out_parts[layer] = owned_out
        gain_parts[layer] = d_gain
        extra_parts[layer] = d_extras
    small_local = (
        jnp.stack(gain_parts),
        jnp.stack([item[0] for item in extra_parts]),
        jnp.stack([item[1] for item in extra_parts]),
        jnp.stack([item[2] for item in extra_parts]),
        jnp.stack([item[3] for item in extra_parts]),
        jnp.stack([item[4] for item in extra_parts]),
        jnp.stack([item[5] for item in extra_parts]),
    )
    summed = lax.psum(
        (
            small_local[0],
            small_local[1],
            small_local[2],
            small_local[3],
            small_local[4],
            small_local[5],
            small_local[6],
        ),
        ("replica", "shard"),
    )
    return (
        hidden.reshape(slot_count, seq_len, width),
        grad_stream.reshape(slot_count, seq_len, width),
        jnp.stack(in_parts),
        jnp.stack(out_parts),
        summed[0],
        summed[1],
        summed[2],
        summed[3],
        summed[4],
        summed[5],
        summed[6],
    )


def solution(mesh):
    in_specs = (
        P(("replica", "shard"), None, None),
        P(("replica", "shard")),
        P(("replica", "shard"), None, None),
        P(None, "shard", None),
        P(None, "shard", None),
        P(),
        P(),
        P(),
        P(),
        P(),
        P(),
        P(),
    )
    out_specs = (
        P(("replica", "shard"), None, None),
        P(("replica", "shard"), None, None),
        P(None, "shard", None),
        P(None, "shard", None),
        P(),
        P(),
        P(),
        P(),
        P(),
        P(),
        P(),
    )
    return jax.shard_map(
        per_device, mesh=mesh, in_specs=in_specs, out_specs=out_specs, check_vma=False
    )
```

profile of v0, /device:TPU:0, one launch (start us, length us, event | category | flops | bytes accessed | tf_op | source)
XLA Modules:
  0.0 2127.9 jit_solution(17221925567403622853)
XLA Ops:
  25.7 68.3 %all-gather.15.cloned.1.call-done = bf16[1,2048,1024]{2,1,0:T(8,128)(2,1)} async-done(((bf16[1,512,1024]{2,1,0:T(8,128)(2,1)}), bf16[1,2048,1024]{2,1,0:T(8,128)(2,1)}) %all-gather.15.cloned.1.call-update) | async-done | bytes 4194320 | tf_op jit(solution)/shard_map/all_gather | solution.py:120
  105.8 147.6 %all-gather.9.cloned.1.call-done = bf16[1,1024,4384]{1,2,0:T(8,128)(2,1)} async-done(((bf16[1,256,4384]{1,2,0:T(8,128)(2,1)}), bf16[1,1024,4384]{1,2,0:T(8,128)(2,1)}) %all-gather.9.cloned.1.call-update) | async-done | bytes 8978448 | tf_op jit(solution)/shard_map/all_gather | solution.py:119
  253.4 17.7 fusion.228
  273.6 195.5 %while.84 = (s32[]{:T(128)}, bf16[2,512,2048]{2,1,0:T(8,128)(2,1)}, f32[1,2304]{1,0:T(1,128)S(1)}, f32[1,2304]{1,0:T(1,128)S(1)}, f32[2,512,4384]{1,2,0:T(8,128)...) while((s32[]{:T(128)}, bf16[2,512,2048]{2,1,0:T(8,128)(2,1)}, ...), condition=%wide.region_5.6_spmd.clone.clone, body=%wide.region_1.5_spmd.clone.clone.sunk | while | flops 5888705024 | bytes 198113264 | solution.py:81
  329.7 20.4 fusion.414
  427.2 20.4 fusion.414
  517.3 439.3 %while.86 = (s32[]{:T(128)}, f32[2304]{0:T(1024)}, f32[4,2304]{1,0:T(4,128)}, f32[32]{0:T(128)}, f32[32]{0:T(128)}, /*index=5*/f32[32]{0:T(128)}, f32[2048]{0:T(...) while((s32[]{:T(128)}, f32[2304]{0:T(1024)}, ...), condition=%wide.region_37.39_spmd.clone, body=%wide.region_12.38_spmd.clone.sunk | while | flops 18517338112 | bytes 734076864 | solution.py:81
  561.6 19.7 bitcast_add_fusion.17
  618.1 26.5 %fusion.456 = (f32[2,32,256]{2,1,0:T(8,128)S(1)}, f32[2,32,256]{2,1,0:T(8,128)}, f32[2,256,256]{2,1,0:T(8,128)S(1)}) fusion(f32[2,256,256]{2,1,0:T(8,128)S(1)} %fusion.452, f32[2,32,256]{2,1,0:T(8,128)S(1)} %get-tuple-element.2367, pred[256,256]{1,0:T(8,128)(4,1)S(1)} %iota_compare_fusion.5, f32[2,256,32,64]{1,0,3,2:T(2,128)} %reshape.1287, ...), kind=kOutput, calls=%fused_computation.112.clone.1 | convolution fusion | flops 3268247552 | bytes 9764864 | tf_op jit(solution)/shard_map/transpose(jvp())/while/body/eval_jaxpr/checkpoint/chqk,ckhp->cqhp/dot_general | solution.py:39
  778.4 19.7 bitcast_add_fusion.17
  834.9 26.5 %fusion.456 = (f32[2,32,256]{2,1,0:T(8,128)S(1)}, f32[2,32,256]{2,1,0:T(8,128)}, f32[2,256,256]{2,1,0:T(8,128)S(1)}) fusion(f32[2,256,256]{2,1,0:T(8,128)S(1)} %fusion.452, f32[2,32,256]{2,1,0:T(8,128)S(1)} %get-tuple-element.2367, pred[256,256]{1,0:T(8,128)(4,1)S(1)} %iota_compare_fusion.5, f32[2,256,32,64]{1,0,3,2:T(2,128)} %reshape.1287, ...), kind=kOutput, calls=%fused_computation.112.clone.1 | convolution fusion | flops 3268247552 | bytes 9764864 | tf_op jit(solution)/shard_map/transpose(jvp())/while/body/eval_jaxpr/checkpoint/chqk,ckhp->cqhp/dot_general | solution.py:39
  998.1 211.0 %while.85 = (s32[]{:T(128)}, bf16[2,512,2048]{2,1,0:T(8,128)(2,1)}, f32[1,2304]{1,0:T(1,128)S(1)}, f32[1,2304]{1,0:T(1,128)S(1)}, f32[2,512,4384]{1,2,0:T(8,128)...) while((s32[]{:T(128)}, bf16[2,512,2048]{2,1,0:T(8,128)(2,1)}, ...), condition=%wide.region_11.12_spmd.clone.clone, body=%wide.region_7.11_spmd.clone.clone.sunk | while | flops 5888705024 | bytes 198113264 | solution.py:81
  1069.9 20.5 fusion.427
  1167.1 20.4 fusion.427
  1253.3 460.2 %while.87 = (s32[]{:T(128)}, f32[2304]{0:T(1024)}, f32[4,2304]{1,0:T(4,128)}, f32[32]{0:T(128)}, f32[32]{0:T(128)}, /*index=5*/f32[32]{0:T(128)}, f32[2048]{0:T(...) while((s32[]{:T(128)}, f32[2304]{0:T(1024)}, ...), condition=%wide.region_64.66_spmd.clone, body=%wide.region_39.65_spmd.clone.sunk | while | flops 18517338112 | bytes 706551744 | solution.py:81
  1307.5 19.7 bitcast_add_fusion.19
  1364.4 26.5 %fusion.488 = (f32[2,32,256]{2,1,0:T(8,128)S(1)}, f32[2,32,256]{2,1,0:T(8,128)}, f32[2,256,256]{2,1,0:T(8,128)S(1)}) fusion(f32[2,256,256]{2,1,0:T(8,128)S(1)} %fusion.484, f32[2,32,256]{2,1,0:T(8,128)S(1)} %get-tuple-element.2434, pred[256,256]{1,0:T(8,128)(4,1)S(1)} %iota_compare_fusion.6, f32[2,256,32,64]{1,0,3,2:T(2,128)} %reshape.1293, ...), kind=kOutput, calls=%fused_computation.257.clone.1 | convolution fusion | flops 3268247552 | bytes 9764864 | tf_op jit(solution)/shard_map/transpose(jvp())/while/body/eval_jaxpr/checkpoint/chqk,ckhp->cqhp/dot_general | solution.py:39
  1534.1 19.7 bitcast_add_fusion.19
  1590.7 26.5 %fusion.488 = (f32[2,32,256]{2,1,0:T(8,128)S(1)}, f32[2,32,256]{2,1,0:T(8,128)}, f32[2,256,256]{2,1,0:T(8,128)S(1)}) fusion(f32[2,256,256]{2,1,0:T(8,128)S(1)} %fusion.484, f32[2,32,256]{2,1,0:T(8,128)S(1)} %get-tuple-element.2434, pred[256,256]{1,0:T(8,128)(4,1)S(1)} %iota_compare_fusion.6, f32[2,256,32,64]{1,0,3,2:T(2,128)} %reshape.1293, ...), kind=kOutput, calls=%fused_computation.257.clone.1 | convolution fusion | flops 3268247552 | bytes 9764864 | tf_op jit(solution)/shard_map/transpose(jvp())/while/body/eval_jaxpr/checkpoint/chqk,ckhp->cqhp/dot_general | solution.py:39
  1729.5 151.6 %reduce-scatter.5.cloned.1.call-done = bf16[256,4384]{0,1:T(8,128)(2,1)} async-done(((bf16[1024,4384]{0,1:T(8,128)(2,1)}), bf16[256,4384]{0,1:T(8,128)(2,1)}) %reduce-scatter.5.cloned.1.call-update) | async-done | bytes 2244624 | tf_op jit(solution)/shard_map/reduce_scatter | solution.py:159
  1893.5 17.5 fusion.244
  1919.4 43.5 %all-reduce.44 = (f32[2,1024]{1,0:T(2,128)}, f32[2,2304]{1,0:T(2,128)}, f32[2,2048]{1,0:T(2,128)}, f32[2,32]{1,0:T(2,128)}, f32[2,32]{1,0:T(2,128)}, /*index=5*/f32[2,32]{1,0:T(2,128)}) all-reduce(f32[2,1024]{1,0:T(2,128)S(1)} %pad_maximum_fusion.3, ...), channel_id=1, replica_groups=mesh['replica'=8,'shard'=4] {'replica','shard'}, use_global_device_ids=true, to_apply=%region_76.78 | all-reduce | flops 10944 | bytes 87552 | tf_op jit(solution)/shard_map/psum | solution.py:183
  1975.6 19.1 all-reduce.51.cloned.1.call-done
  2003.6 115.4 %all-reduce.49.cloned.1.call-done = f32[2,4,2304]{2,1,0:T(4,128)} async-done(((f32[2,4,2304]{2,1,0:T(4,128)}), f32[2,4,2304]{2,1,0:T(4,128)}) %all-reduce.49.cloned.1.call-update) | async-done | bytes 73744 | tf_op jit(solution)/shard_map/psum | solution.py:183
  (1113 shorter events, 1230.1 us)
Async XLA Ops:
  7.2 86.8 %all-gather.15.cloned.1.call-start = ((), (), s32[]{:S(2)}) async-start(), calls=%async_computation.12 | async-start | bytes 5242880 | tf_op jit(solution)/shard_map/all_gather | solution.py:120
  10.3 243.1 %all-gather.9.cloned.1.call-start = ((), (), s32[]{:S(2)}) async-start(), calls=%async_computation.9 | async-start | bytes 11223040 | tf_op jit(solution)/shard_map/all_gather | solution.py:119
  15.2 454.0 %all-gather.11.cloned.1.call-start = ((), (), s32[]{:S(2)}) async-start(), calls=%async_computation.10 | async-start | bytes 5242880 | tf_op jit(solution)/shard_map/all_gather | solution.py:120
  15.9 476.8 %all-gather.13.cloned.1.call-start = ((), (), s32[]{:S(2)}) async-start(), calls=%async_computation.11 | async-start | bytes 11223040 | tf_op jit(solution)/shard_map/all_gather | solution.py:119
  16.5 1712.9 %reduce-scatter.9.cloned.1.call-start = ((), (), s32[]{:S(2)}) async-start(), calls=%async_computation.6 | async-start | bytes 5242880 | tf_op jit(solution)/shard_map/reduce_scatter | solution.py:162
  18.5 234.9 %copy-start.121 = (f32[1,1024]{1,0:T(1,128)}, f32[1,1024]{1,0:T(1,128)S(1)}, u32[]{:S(2)}) copy-start(f32[1,1024]{1,0:T(1,128)S(1)} %get-tuple-element.1838) | copy-start | bytes 12292
  22.0 231.4 %copy-start.131 = (f32[2,512]{1,0:T(2,128)}, f32[2,512]{1,0:T(2,128)S(1)}, u32[]{:S(2)}) copy-start(f32[2,512]{1,0:T(2,128)S(1)} %get-tuple-element.1840) | copy-start | bytes 12292
  24.5 81.3 %copy-start.136 = (f32[2,512]{1,0:T(2,128)}, f32[2,512]{1,0:T(2,128)S(1)}, u32[]{:S(2)}) copy-start(f32[2,512]{1,0:T(2,128)S(1)} %get-tuple-element.1853) | copy-start | bytes 12292
  273.6 195.6 %copy-start.132 = (f32[1,4,2,128]{3,1,2,0:T(4,128)S(1)}, f32[1,4,2,128]{3,1,2,0:T(4,128)}, u32[]{:S(2)}) copy-start(f32[1,4,2,128]{3,1,2,0:T(4,128)} %copy.386) | copy-start | bytes 12292
  541.4 76.8 %copy-start.40 = (f32[2,32,256]{2,1,0:T(8,128)}, f32[2,32,256]{2,1,0:T(8,128)S(1)}, u32[]{:S(2)}) copy-start(f32[2,32,256]{2,1,0:T(8,128)S(1)} %get-tuple-element.2367) | copy-start | bytes 196612 | tf_op jit(solution)/shard_map/transpose(jvp())/while
  561.6 56.5 %copy-start.44 = (pred[256,256]{1,0:T(8,128)(4,1)}, pred[256,256]{1,0:T(8,128)(4,1)S(1)}, u32[]{:S(2)}) copy-start(pred[256,256]{1,0:T(8,128)(4,1)S(1)} %iota_compare_fusion.5) | copy-start | bytes 196612 | tf_op jit(solution)/shard_map/transpose(jvp())/while
  758.1 76.8 %copy-start.40 = (f32[2,32,256]{2,1,0:T(8,128)}, f32[2,32,256]{2,1,0:T(8,128)S(1)}, u32[]{:S(2)}) copy-start(f32[2,32,256]{2,1,0:T(8,128)S(1)} %get-tuple-element.2367) | copy-start | bytes 196612 | tf_op jit(solution)/shard_map/transpose(jvp())/while
  778.4 56.5 %copy-start.44 = (pred[256,256]{1,0:T(8,128)(4,1)}, pred[256,256]{1,0:T(8,128)(4,1)S(1)}, u32[]{:S(2)}) copy-start(pred[256,256]{1,0:T(8,128)(4,1)S(1)} %iota_compare_fusion.5) | copy-start | bytes 196612 | tf_op jit(solution)/shard_map/transpose(jvp())/while
  995.5 734.0 %reduce-scatter.11.cloned.1.call-start = ((), (), s32[]{:S(2)}) async-start(), calls=%async_computation.7 | async-start | bytes 5242880 | tf_op jit(solution)/shard_map/reduce_scatter | solution.py:162
  998.1 211.0 %copy-start.137 = (f32[2,512]{1,0:T(2,128)S(1)}, f32[2,512]{1,0:T(2,128)}, u32[]{:S(2)}) copy-start(f32[2,512]{1,0:T(2,128)} %copy-done.136) | copy-start | bytes 12292
  1219.3 510.2 %reduce-scatter.7.cloned.1.call-start = ((), (), s32[]{:S(2)}) async-start(), calls=%async_computation.5 | async-start | bytes 11223040 | tf_op jit(solution)/shard_map/reduce_scatter | solution.py:159
  1237.1 644.0 %reduce-scatter.5.cloned.1.call-start = ((), (), s32[]{:S(2)}) async-start(), calls=%async_computation.4 | async-start | bytes 11223040 | tf_op jit(solution)/shard_map/reduce_scatter | solution.py:159
  1287.2 77.2 %copy-start.42 = (f32[2,32,256]{2,1,0:T(8,128)}, f32[2,32,256]{2,1,0:T(8,128)S(1)}, u32[]{:S(2)}) copy-start(f32[2,32,256]{2,1,0:T(8,128)S(1)} %get-tuple-element.2434) | copy-start | bytes 196612 | tf_op jit(solution)/shard_map/transpose(jvp())/while
  1307.5 56.9 %copy-start.46 = (pred[256,256]{1,0:T(8,128)(4,1)}, pred[256,256]{1,0:T(8,128)(4,1)S(1)}, u32[]{:S(2)}) copy-start(pred[256,256]{1,0:T(8,128)(4,1)S(1)} %iota_compare_fusion.6) | copy-start | bytes 196612 | tf_op jit(solution)/shard_map/transpose(jvp())/while
  1513.9 76.8 %copy-start.42 = (f32[2,32,256]{2,1,0:T(8,128)}, f32[2,32,256]{2,1,0:T(8,128)S(1)}, u32[]{:S(2)}) copy-start(f32[2,32,256]{2,1,0:T(8,128)S(1)} %get-tuple-element.2434) | copy-start | bytes 196612 | tf_op jit(solution)/shard_map/transpose(jvp())/while
  1534.1 56.6 %copy-start.46 = (pred[256,256]{1,0:T(8,128)(4,1)}, pred[256,256]{1,0:T(8,128)(4,1)S(1)}, u32[]{:S(2)}) copy-start(pred[256,256]{1,0:T(8,128)(4,1)S(1)} %iota_compare_fusion.6) | copy-start | bytes 196612 | tf_op jit(solution)/shard_map/transpose(jvp())/while
  1729.3 151.8 %copy-start.126 = (f32[1,4,2,128]{3,2,1,0:T(2,128)S(1)}, f32[1,4,2,128]{3,2,1,0:T(2,128)}, u32[]{:S(2)}) copy-start(f32[1,4,2,128]{3,2,1,0:T(2,128)} %get-tuple-element.1839) | copy-start | bytes 12292
  1729.3 265.4 %all-reduce.51.cloned.1.call-start = ((), (), s32[]{:S(2)}) async-start(), calls=%async_computation.13 | async-start | bytes 13172736 | tf_op jit(solution)/shard_map/psum | solution.py:167
  1881.1 237.9 %all-reduce.49.cloned.1.call-start = ((), (), s32[]{:S(2)}) async-start(), calls=%async_computation.8 | async-start | bytes 147456 | tf_op jit(solution)/shard_map/psum | solution.py:183
  (252 other events, 1479.2 us)
Sparse Core Ops, SparseCore 0:
  10.5 83.4 all-gather.14
  96.1 157.2 all-gather.8
  255.0 78.9 all-gather.10
  335.4 157.2 all-gather.12
  995.6 74.9 reduce-scatter.8
  1219.4 74.9 reduce-scatter.10
  1296.8 154.2 reduce-scatter.6
  1729.5 151.6 reduce-scatter.4
  1884.9 109.7 all-reduce.50
  2000.7 118.3 all-reduce.48
where the time goes:
time: 2140 us; the launch traced here: 2130 us
  matrix products  669 us (31%)
  waiting for transfers between devices  516 us (24%)
  other arithmetic  425 us (20%)
  local copies, waits for them, and re-layouts  424 us (20%)
  blocking collectives  43.5 us (2%)
  loops' own time  34.9 us (2%)
    dot_general x16, matrix products, span_scan(): intra = jnp.einsum('chqk,ckhp->cqhp', mixing, scaled_x, precision=HIGHEST)  327 us
    all_gather x2, waiting for transfers between devices, per_device(): lax.all_gather(w_in[layer], 'shard', axis=0, tiled=True)  160 us
    reduce_scatter x2, waiting for transfers between devices, per_device(): lax.psum_scatter(local_in.astype(jnp.bfloat16), 'shard', scatter_dimensio...  152 us
    psum x1, waiting for transfers between devices, per_device(): lax.psum((small_local[0], small_local[1], small_local[2], small_local[3],...  115 us
    mul x8, other arithmetic, mix_one(): act = jax.nn.silu(pre_act)  83.6 us
    while x416, local copies, waits for them, and re-layouts  80.3 us
    all_gather x2, waiting for transfers between devices, per_device(): lax.all_gather(w_out[layer], 'shard', axis=0, tiled=True)  68.3 us
    mul x20, other arithmetic, mix_one(): conv_weight[offset][None, :] * padded[offset:offset + seq_len]  67.5 us
  transfers between devices with their start and end apart: 10, of which 6 were waited for; matrix products, arithmetic and copies ran while one was open for 46% of the time, Pallas kernels for 0%

commit v1 on v0

v1 whole, which is shorter than its diff:
```python
import jax
import jax.numpy as jnp
from jax import lax
from jax.experimental import pallas as pl
from jax.experimental.pallas import tpu as pltpu
from jax.sharding import Mesh
from jax.sharding import PartitionSpec as P

DI = 2048
HEADS = 32
HEAD_DIM = 64
STATE = 128
CONV = 4
EPSILON = 1e-05
CHUNK = 128
PAIR = 2 * HEAD_DIM
LOG2E = 1.4426950408889634
BF = jnp.bfloat16
F32 = jnp.float32


def dot_f32(left, right, dims, precision=None):
    return lax.dot_general(
        left, right, (dims, ((), ())), preferred_element_type=F32, precision=precision
    )


def mm(left, right):
    return dot_f32(left, right, ((1,), (0,)))


def mm_nt(left, right):
    return dot_f32(left, right, ((1,), (1,)))


def mm_tn(left, right):
    return dot_f32(left, right, ((0,), (0,)))


def split_two(values):
    high = values.astype(BF)
    low = (values - high.astype(F32)).astype(BF)
    return high, low


def block_diag(pair):
    lane = lax.broadcasted_iota(jnp.int32, pair.shape, 1)
    zero = jnp.zeros_like(pair)
    return jnp.concatenate(
        [jnp.where(lane < HEAD_DIM, pair, zero), jnp.where(lane >= HEAD_DIM, pair, zero)], axis=0
    )


def sigmoid(values):
    return 1.0 / (1.0 + jnp.exp(-values))


def softplus(values):
    return jnp.maximum(values, 0.0) + jnp.log1p(jnp.exp(-jnp.abs(values)))


def conv_pre(ext_ref, cw_ref, cb_ref, cols):
    total = cb_ref[:, cols] + cw_ref[0:1, cols] * ext_ref[5 : 5 + CHUNK, cols]
    for tap in range(1, CONV):
        total = total + cw_ref[tap : tap + 1, cols] * ext_ref[5 + tap : 5 + tap + CHUNK, cols]
    return total


def head_terms(raw_ref, dtb_ref, al_ref, spread_ref):
    shifted = raw_ref[...] + dtb_ref[...]
    step = softplus(shifted)
    rate = -jnp.exp(al_ref[...])
    row = lax.broadcasted_iota(jnp.int32, (CHUNK, CHUNK), 0)
    col = lax.broadcasted_iota(jnp.int32, (CHUNK, CHUNK), 1)
    lower = (row >= col).astype(F32)
    cum = dot_f32(lower, step * (rate * LOG2E), ((1,), (0,)), lax.Precision.HIGHEST)
    to_end = jnp.exp2(cum[CHUNK - 1 : CHUNK, :] - cum)

    def spread(values):
        high, low = split_two(values)
        return mm(jnp.concatenate([high, low], axis=1), spread_ref[...])

    return shifted, step, rate, cum, spread(step), spread(to_end), spread(jnp.exp2(cum))


def fwd_body(
    proj_ref, raw_ref, cw_ref, cb_ref, gg_ref, dtb_ref, al_ref, sk_ref, spread_ref,
    mixed_ref, y_ref, entry_ref,
    state, ext, gated,
):
    chunk = pl.program_id(1)

    @pl.when(chunk == 0)
    def _():
        state[...] = jnp.zeros_like(state)
        ext[0:8, :] = jnp.zeros((8, ext.shape[1]), F32)

    @pl.when(chunk != 0)
    def _():
        ext[0:8, :] = ext[CHUNK : CHUNK + 8, :]

    ext[8 : 8 + CHUNK, :] = proj_ref[:, DI : 2 * DI + 2 * STATE].astype(F32)

    def act(start, width):
        pre = conv_pre(ext, cw_ref, cb_ref, slice(start, start + width))
        return pre * sigmoid(pre)

    b_low = act(DI, STATE).astype(BF)
    c_low = act(DI + STATE, STATE).astype(BF)
    _, _, _, cum, step_x, end_x, ecum_x = head_terms(raw_ref, dtb_ref, al_ref, spread_ref)
    cum_t = cum.T
    row = lax.broadcasted_iota(jnp.int32, (CHUNK, CHUNK), 0)
    col = lax.broadcasted_iota(jnp.int32, (CHUNK, CHUNK), 1)
    scores = jnp.where(row >= col, mm_nt(c_low, b_low), 0.0)
    entry_low = state[...].astype(BF)
    entry_ref[0] = entry_low
    b_t = b_low.astype(F32).T.astype(BF)
    squares = jnp.zeros((CHUNK, PAIR), F32)
    for pair in range(HEADS // 2):
        cols = slice(pair * PAIR, (pair + 1) * PAIR)
        x = act(pair * PAIR, PAIR)
        x_step = x * step_x[:, cols]
        mixing = []
        for head in (2 * pair, 2 * pair + 1):
            gap = jnp.minimum(cum[:, head : head + 1] - cum_t[head : head + 1, :], 0.0)
            mixing.append((jnp.exp2(gap) * scores).astype(BF))
        intra = mm(jnp.concatenate(mixing, axis=1), block_diag(x_step.astype(BF)))
        inter = mm(c_low, entry_low[:, cols]) * ecum_x[:, cols]
        y = intra + inter + sk_ref[:, cols] * x
        y_ref[:, cols] = y.astype(BF)
        grown = mm(b_t, (x_step * end_x[:, cols]).astype(BF))
        state[:, cols] = state[:, cols] * ecum_x[CHUNK - 1 : CHUNK, cols] + grown
        z = proj_ref[:, cols].astype(F32)
        g = y * (z * sigmoid(z))
        gated[:, cols] = g
        squares = squares + g * g
    scale = lax.rsqrt(jnp.sum(squares, axis=1, keepdims=True) * (1.0 / DI) + EPSILON)
    for pair in range(HEADS // 2):
        cols = slice(pair * PAIR, (pair + 1) * PAIR)
        mixed_ref[:, cols] = (gated[:, cols] * scale * gg_ref[:, cols]).astype(BF)


def bwd_body(
    proj_ref, before_ref, raw_ref, y_ref, entry_ref, dmix_ref,
    cw_ref, cb_ref, gg_ref, dtb_ref, al_ref, sk_ref, spread_ref, gather_ref,
    cw0_ref, cb0_ref, gg0_ref, sk0_ref, dtb0_ref, al0_ref,
    dproj_ref, dcw_ref, dcb_ref, dgg_ref, dsk_ref, ddtb_ref, dal_ref,
    adj, ext, dpre, act_s, slope_s, dy_s, da_high, da_low, u_s,
):
    turn = pl.program_id(0)
    last = pl.num_programs(0) - 1

    @pl.when(turn == 0)
    def _():
        dcw_ref[...] = cw0_ref[...]
        dcb_ref[...] = cb0_ref[...]
        dgg_ref[...] = gg0_ref[...]
        dsk_ref[...] = sk0_ref[...]
        ddtb_ref[...] = dtb0_ref[...]
        dal_ref[...] = al0_ref[...]

    @pl.when(turn == 0)
    def _():
        adj[...] = jnp.zeros_like(adj)
        dpre[CHUNK : CHUNK + 8, :] = jnp.zeros((8, dpre.shape[1]), F32)

    ext[0:8, :] = jnp.where(
        turn == last, 0.0, before_ref[8:16, DI : 2 * DI + 2 * STATE].astype(F32)
    )
    ext[8 : 8 + CHUNK, :] = proj_ref[:, DI : 2 * DI + 2 * STATE].astype(F32)
    conv_width = DI + 2 * STATE
    for start in range(0, conv_width, PAIR):
        cols = slice(start, start + PAIR)
        pre = conv_pre(ext, cw_ref, cb_ref, cols)
        sig = sigmoid(pre)
        act = pre * sig
        act_s[:, cols] = act
        slope_s[:, cols] = sig + act * (1.0 - sig)

    squares = jnp.zeros((CHUNK, PAIR), F32)
    crossed = jnp.zeros((CHUNK, PAIR), F32)
    for pair in range(HEADS // 2):
        cols = slice(pair * PAIR, (pair + 1) * PAIR)
        z = proj_ref[:, cols].astype(F32)
        g = y_ref[:, cols].astype(F32) * (z * sigmoid(z))
        squares = squares + g * g
        crossed = crossed + dmix_ref[:, cols].astype(F32) * gg_ref[:, cols] * g
    scale = lax.rsqrt(jnp.sum(squares, axis=1, keepdims=True) * (1.0 / DI) + EPSILON)
    pull = scale * scale * scale * (jnp.sum(crossed, axis=1, keepdims=True) * (1.0 / DI))
    for pair in range(HEADS // 2):
        cols = slice(pair * PAIR, (pair + 1) * PAIR)
        z = proj_ref[:, cols].astype(F32)
        y = y_ref[:, cols].astype(F32)
        d_mixed = dmix_ref[:, cols].astype(F32)
        sig = sigmoid(z)
        silu = z * sig
        g = y * silu
        scaled = d_mixed * scale
        d_gated = scaled * gg_ref[:, cols] - g * pull
        dgg_ref[:, cols] += jnp.sum(scaled * g, axis=0, keepdims=True)
        dy_s[:, cols] = d_gated * silu
        dproj_ref[:, cols] = (d_gated * y * (sig + silu * (1.0 - sig))).astype(BF)

    b_low = act_s[:, DI : DI + STATE].astype(BF)
    c_low = act_s[:, DI + STATE :].astype(BF)
    shifted, step, rate, cum, step_x, end_x, ecum_x = head_terms(
        raw_ref, dtb_ref, al_ref, spread_ref
    )
    cum_t = cum.T
    row = lax.broadcasted_iota(jnp.int32, (CHUNK, CHUNK), 0)
    col = lax.broadcasted_iota(jnp.int32, (CHUNK, CHUNK), 1)
    raw_scores = mm_nt(c_low, b_low)
    scores = jnp.where(row >= col, raw_scores, 0.0)
    scores_t = scores.T
    c_t = c_low.astype(F32).T.astype(BF)
    d_scores = jnp.zeros((CHUNK, CHUNK), F32)
    d_c = jnp.zeros((CHUNK, STATE), F32)
    d_b = jnp.zeros((CHUNK, STATE), F32)
    crossing = []
    for pair in range(HEADS // 2):
        cols = slice(pair * PAIR, (pair + 1) * PAIR)
        x = act_s[:, cols]
        dy = dy_s[:, cols]
        step_p = step_x[:, cols]
        x_step = x * step_p
        x_low = x_step.astype(BF)
        dy_low = dy.astype(BF)
        x_bd = block_diag(x_low)
        g_both = mm_nt(dy_low, x_bd)
        mixing = []
        mixing_t = []
        for place, head in enumerate((2 * pair, 2 * pair + 1)):
            down = cum[:, head : head + 1]
            across = cum_t[head : head + 1, :]
            decay = jnp.exp2(jnp.minimum(down - across, 0.0))
            mixing.append((decay * scores).astype(BF))
            d_scores = d_scores + decay * g_both[:, place * CHUNK : (place + 1) * CHUNK]
            decay_t = jnp.exp2(jnp.minimum(across - down, 0.0))
            mixing_t.append((decay_t * scores_t).astype(BF))
        intra = mm(jnp.concatenate(mixing, axis=1), x_bd)
        spread_dy = mm(jnp.concatenate(mixing_t, axis=1), block_diag(dy_low))
        entry = entry_ref[0, :, cols]
        adj_p = adj[:, cols]
        adj_low = adj_p.astype(BF)
        ecum_p = ecum_x[:, cols]
        end_p = end_x[:, cols]
        from_end = mm(b_low, adj_low) * end_p
        y_scan = intra + mm(c_low, entry) * ecum_p
        stuff = spread_dy + from_end
        x_round = x_low.astype(F32)
        u = x_round * stuff
        high, low = split_two(dy_low.astype(F32) * y_scan - u)
        da_high[:, cols] = high
        da_low[:, cols] = low
        u_s[:, cols] = u.astype(BF)
        dy_e = (dy * ecum_p).astype(BF)
        x_e = (x_step * end_p).astype(BF)
        d_c = d_c + mm_nt(dy_e, entry)
        d_b = d_b + mm_nt(x_e, adj_low)
        ecum_last = ecum_x[CHUNK - 1 : CHUNK, cols]
        crossing.append(
            jnp.sum(x_round * from_end, axis=0, keepdims=True)
            + ecum_last * jnp.sum(adj_p * entry.astype(F32), axis=0, keepdims=True)
        )
        adj[:, cols] = adj_p * ecum_last + mm(c_t, dy_e)
        dsk_ref[:, cols] += jnp.sum(dy * x, axis=0, keepdims=True)
        dpre[0:CHUNK, cols] = (step_p * stuff + sk_ref[:, cols] * dy) * slope_s[:, cols]

    through = mm(da_high[...], gather_ref[...]) + mm(da_low[...], gather_ref[...])
    u_head = mm(u_s[...], gather_ref[...])[:, :HEADS]
    cross_row = jnp.broadcast_to(jnp.concatenate(crossing, axis=1), (16, DI))
    cross_high, cross_low = split_two(cross_row)
    cross = (mm(cross_high, gather_ref[...]) + mm(cross_low, gather_ref[...]))[0:1, :HEADS]
    upper = (row <= col).astype(F32)
    d_log = dot_f32(upper, through[:, :HEADS], ((1,), (0,)), lax.Precision.HIGHEST) + cross
    sig = sigmoid(shifted)
    ratio = jnp.where(step > 1e-30, sig / step, 1.0)
    d_raw = u_head * ratio + rate * d_log * sig
    dproj_ref[:, 2 * DI + 2 * STATE :] = d_raw.astype(BF)
    ddtb_ref[...] += jnp.sum(d_raw, axis=0, keepdims=True)
    dal_ref[...] += rate * jnp.sum(step * d_log, axis=0, keepdims=True)

    d_scores = jnp.where(row >= col, d_scores, 0.0)
    d_c = d_c + mm(d_scores.astype(BF), b_low)
    d_b = d_b + mm(d_scores.T.astype(BF), c_low)
    dpre[0:CHUNK, DI : DI + STATE] = d_b * slope_s[:, DI : DI + STATE]
    dpre[0:CHUNK, DI + STATE :] = d_c * slope_s[:, DI + STATE :]
    for start in range(0, conv_width, PAIR):
        cols = slice(start, start + PAIR)
        here = dpre[0:CHUNK, cols]
        d_conv = cw_ref[CONV - 1 : CONV, cols] * here
        dcb_ref[:, cols] += jnp.sum(here, axis=0, keepdims=True)
        for tap in range(CONV):
            dcw_ref[tap : tap + 1, cols] += jnp.sum(
                here * ext[5 + tap : 5 + tap + CHUNK, cols], axis=0, keepdims=True
            )
            if tap < CONV - 1:
                ahead = CONV - 1 - tap
                d_conv = d_conv + cw_ref[tap : tap + 1, cols] * dpre[ahead : ahead + CHUNK, cols]
        dproj_ref[:, DI + start : DI + start + PAIR] = d_conv.astype(BF)
    dpre[CHUNK : CHUNK + 8, :] = dpre[0:8, :]


def head_maps():
    head = jnp.arange(DI) // HEAD_DIM
    spread = (jnp.arange(HEADS)[:, None] == head[None, :]).astype(BF)
    gather = (head[:, None] == jnp.arange(128)[None, :]).astype(BF)
    return jnp.concatenate([spread, spread], axis=0), gather


def whole(array):
    return pl.BlockSpec(array.shape, lambda seq, turn: (0,) * array.ndim)


def param_rows(extras):
    conv_weight, conv_bias, gate_gain, dt_bias, a_log, skip = extras
    return (
        conv_weight,
        conv_bias[None, :],
        gate_gain[None, :],
        dt_bias[None, :],
        a_log[None, :],
        jnp.repeat(skip, HEAD_DIM)[None, :],
    )


def mix_forward(proj, raw, extras, seq_len):
    rows = proj.shape[0]
    seqs, chunks = rows // seq_len, seq_len // CHUNK
    params = param_rows(extras) + (head_maps()[0],)

    def at(width):
        return pl.BlockSpec((CHUNK, width), lambda seq, turn: (seq * chunks + turn, 0))

    conv_width = DI + 2 * STATE
    return pl.pallas_call(
        fwd_body,
        grid=(seqs, chunks),
        in_specs=[at(proj.shape[1]), at(HEADS)] + [whole(item) for item in params],
        out_specs=[
            at(DI),
            at(DI),
            pl.BlockSpec((1, STATE, DI), lambda seq, turn: (seq * chunks + turn, 0, 0)),
        ],
        out_shape=[
            jax.ShapeDtypeStruct((rows, DI), BF),
            jax.ShapeDtypeStruct((rows, DI), BF),
            jax.ShapeDtypeStruct((rows // CHUNK, STATE, DI), BF),
        ],
        scratch_shapes=[
            pltpu.VMEM((STATE, DI), F32),
            pltpu.VMEM((CHUNK + 8, conv_width), F32),
            pltpu.VMEM((CHUNK, DI), F32),
        ],
        compiler_params=pltpu.CompilerParams(
            dimension_semantics=("arbitrary", "arbitrary"), vmem_limit_bytes=48 << 20
        ),
        cost_estimate=pl.CostEstimate(
            flops=30 * rows * DI * 512, bytes_accessed=rows * 24 * 1024, transcendentals=rows * DI
        ),
        name="mix_forward",
    )(proj, raw, *params)


def mix_backward(proj, raw, y, entry, d_mixed, extras, seq_len, seq, earlier, sums):
    rows = proj.shape[0]
    chunks = seq_len // CHUNK
    params = param_rows(extras) + head_maps()
    conv_width = DI + 2 * STATE
    per = CHUNK // 16

    def block(turn):
        return seq * chunks + chunks - 1 - turn

    def at(width):
        return pl.BlockSpec((CHUNK, width), lambda turn: (block(turn), 0))

    def fixed(shape):
        return pl.BlockSpec(shape, lambda turn: (0,) * len(shape))

    small = [(CONV, conv_width), (1, conv_width), (1, DI), (1, DI), (1, HEADS), (1, HEADS)]
    if sums is None:
        sums = [jnp.zeros(shape, F32) for shape in small]
    operands = [proj, proj, raw, y, entry, d_mixed, *params, *sums]
    in_specs = [
        at(proj.shape[1]),
        pl.BlockSpec(
            (16, proj.shape[1]), lambda turn: (jnp.maximum(block(turn) * per - 1, 0), 0)
        ),
        at(HEADS),
        at(DI),
        pl.BlockSpec((1, STATE, DI), lambda turn: (block(turn), 0, 0)),
        at(DI),
    ]
    in_specs += [fixed(item.shape) for item in params + tuple(sums)]
    aliases = {len(operands) - len(small) + k: 1 + k for k in range(len(small))}
    body = bwd_body
    if earlier is not None:
        aliases[len(operands)] = 0
        operands.append(earlier)
        in_specs.append(pl.BlockSpec(memory_space=pl.ANY))
    count = len(operands)

    def run(*refs):
        fixed_count = 6 + len(params)
        bwd_body(*refs[: fixed_count + len(small)], *refs[count:])

    d_proj, *sums = pl.pallas_call(
        run,
        grid=(chunks,),
        in_specs=in_specs,
        out_specs=[at(proj.shape[1])] + [fixed(shape) for shape in small],
        out_shape=[jax.ShapeDtypeStruct(proj.shape, BF)]
        + [jax.ShapeDtypeStruct(shape, F32) for shape in small],
        input_output_aliases=aliases,
        scratch_shapes=[
            pltpu.VMEM((STATE, DI), F32),
            pltpu.VMEM((CHUNK + 8, conv_width), F32),
            pltpu.VMEM((CHUNK + 8, conv_width), F32),
            pltpu.VMEM((CHUNK, conv_width), F32),
            pltpu.VMEM((CHUNK, conv_width), F32),
            pltpu.VMEM((CHUNK, DI), F32),
            pltpu.VMEM((CHUNK, DI), BF),
            pltpu.VMEM((CHUNK, DI), BF),
            pltpu.VMEM((CHUNK, DI), BF),
        ],
        compiler_params=pltpu.CompilerParams(
            dimension_semantics=("arbitrary",), vmem_limit_bytes=48 << 20
        ),
        cost_estimate=pl.CostEstimate(
            flops=70 * seq_len * DI * 512,
            bytes_accessed=seq_len * 40 * 1024,
            transcendentals=seq_len * DI,
        ),
        name="mix_backward",
    )(*operands)
    return d_proj, sums


def rms_scale(values, gain):
    return values * lax.rsqrt(jnp.mean(values * values, axis=-1, keepdims=True) + EPSILON) * gain


def norm_back(values, gain, d_normed):
    scale = lax.rsqrt(jnp.mean(values * values, axis=-1, keepdims=True) + EPSILON)
    scaled = values * scale
    pulled = d_normed * gain
    d_gain = jnp.sum(d_normed * scaled, axis=0)
    d_values = scale * (pulled - scaled * jnp.mean(pulled * scaled, axis=-1, keepdims=True))
    return d_values, d_gain


def tie(*values):
    return lax.optimization_barrier(values)


def gather_rows(shard_rows):
    parts = lax.axis_size("chip") * lax.axis_size("core")
    place = lax.axis_index("chip") * lax.axis_size("core") + lax.axis_index("core")
    count = shard_rows.shape[0] // parts
    mine = lax.dynamic_slice_in_dim(shard_rows, place * count, count, 0)
    return lax.all_gather(mine, ("shard", "chip", "core"), axis=0, tiled=True)


def flip(value, axis, bit=1):
    count = lax.axis_size(axis)
    return lax.ppermute(value, axis, [(place, place ^ bit) for place in range(count)])


def turn(value, axis, shift):
    count = lax.axis_size(axis)
    return lax.ppermute(value, axis, [(place, (place + shift) % count) for place in range(count)])


def add_low(left, right):
    return (left.astype(F32) + right.astype(F32)).astype(BF)


def core_halves(left):
    half = left.shape[1] // lax.axis_size("shard") // 2
    first = lax.axis_index("core") == 0

    def pick(low_first):
        pieces = []
        for start in range(0, left.shape[1], 2 * half):
            low, high = left[:, start : start + half], left[:, start + half : start + 2 * half]
            pieces.append(jnp.where(low_first, low, high))
        return jnp.concatenate(pieces, axis=1)

    return pick(first), pick(~first)


def chip_bits():
    return [1 << k for k in reversed(range(lax.axis_size("chip").bit_length() - 1))]


def spread_blocks(part):
    bits = chip_bits()
    shards = lax.axis_size("shard")
    rows = part.shape[0] // shards >> len(bits)
    return part.reshape((shards,) + (2,) * len(bits) + (rows, part.shape[1]))


def halve(part, bit):
    axis = 1 + chip_bits().index(bit)
    mine = (lax.axis_index("chip") // bit) % 2
    keep = lax.dynamic_index_in_dim(part, mine, axis)
    send = lax.dynamic_index_in_dim(part, 1 - mine, axis)
    return keep, send


class Stages:
    def __init__(self, steps):
        self.steps = steps
        self.sent = next(steps)
        self.result = None

    def advance(self, main):
        if self.sent is None:
            return main
        main, *arrived = tie(main, *self.sent)
        try:
            ready = self.steps.send(arrived)
            main, *ready = tie(main, *ready)
            self.sent = self.steps.send(ready)
        except StopIteration as stop:
            self.sent, self.result = None, stop.value
        return main

    def finish(self):
        while self.sent is not None:
            try:
                ready = self.steps.send(list(self.sent))
                self.sent = self.steps.send(ready)
            except StopIteration as stop:
                self.sent, self.result = None, stop.value
        return self.result


def sum_columns(keeps, sends):
    bits = chip_bits()
    middle = len(bits) // 2
    orders = (bits, bits[middle:] + bits[:middle])
    arrived = yield [flip(send, "core") for send in sends]
    parts = [spread_blocks(add_low(keep, other)) for keep, other in zip(keeps, arrived)]
    for turn_bits in zip(*orders):
        pieces = [halve(part, bit) for part, bit in zip(parts, turn_bits)]
        ready = yield [send for _, send in pieces]
        arrived = yield [flip(send, "chip", bit) for send, bit in zip(ready, turn_bits)]
        parts = [add_low(keep, other) for (keep, _), other in zip(pieces, arrived)]
    shards = lax.axis_size("shard")
    place = lax.axis_index("shard")
    blocks = [part.reshape(shards, -1, part.shape[-1]) for part in parts]

    def block(value, index):
        return lax.dynamic_index_in_dim(value, index % shards, 0, keepdims=False)

    away = [block(value, place + shift) for value in blocks for shift in range(1, shards)]
    ready = yield away
    shifts = [shift for _ in blocks for shift in range(1, shards)]
    arrived = yield [turn(value, "shard", shift) for value, shift in zip(ready, shifts)]
    owned = []
    for k, value in enumerate(blocks):
        total = block(value, place).astype(F32)
        for other in arrived[k * (shards - 1) : (k + 1) * (shards - 1)]:
            total = total + other.astype(F32)
        owned.append(total.astype(BF))
    owned = jnp.concatenate(owned, axis=1)
    return lax.all_gather(owned, ("core", "chip"), axis=0, tiled=True)


def sum_rows(keep, send):
    part = add_low(keep, flip(send, "core"))
    owned = lax.psum_scatter(part, ("shard", "chip"), scatter_dimension=0, tiled=True)
    return lax.all_gather(owned, ("core", "chip"), axis=0, tiled=True)


def sum_everywhere(values):
    sizes = [value.size for value in values]
    flat = jnp.concatenate([value.reshape(-1) for value in values])
    packed = jnp.pad(flat, (0, -flat.size % 1024)).reshape(-1, 128)
    for axis in ("core", "chip", "shard"):
        arrived = [turn(packed, axis, shift) for shift in range(1, lax.axis_size(axis))]
        packed = sum(arrived, packed)
    flat = packed.reshape(-1)
    out, start = [], 0
    for value, size in zip(values, sizes):
        out.append(flat[start : start + size].reshape(value.shape))
        start += size
    return out


def per_device(
    inputs,
    lengths,
    cotangent,
    w_in,
    w_out,
    norm_gain,
    conv_weight,
    conv_bias,
    gate_gain,
    dt_bias,
    a_log,
    skip,
):
    slot_count, seq_len, width = inputs.shape
    row_total = slot_count * seq_len
    places = lax.broadcasted_iota(jnp.int32, (slot_count, seq_len), 1)
    valid_mask = (places < lengths[:, None]).astype(F32).reshape(row_total, 1)
    layer_count = w_in.shape[0]
    raw_start = 2 * DI + 2 * STATE
    full = [(gather_rows(w_in[layer]), gather_rows(w_out[layer])) for layer in range(layer_count)]
    hidden = inputs.reshape(row_total, width)
    saved = []
    for layer in range(layer_count):
        full_in, full_out = full[layer]
        extras = tuple(
            item[layer] for item in (conv_weight, conv_bias, gate_gain, dt_bias, a_log, skip)
        )
        normed = rms_scale(hidden, norm_gain[layer]).astype(BF)
        proj = mm(normed, full_in).astype(BF)
        raw = mm(normed, full_in[:, raw_start:])
        mixed, y, entry = mix_forward(proj, raw, extras, seq_len)
        saved.append((hidden, normed, proj, raw, mixed, y, entry, extras))
        hidden = hidden + valid_mask * mm(mixed, full_out)
    grad_stream = cotangent.reshape(row_total, width)
    grad_stream, mixed_last = tie(grad_stream, saved[-1][4])
    saved[-1] = saved[-1][:4] + (mixed_last,) + saved[-1][5:]
    in_parts = [None] * layer_count
    out_parts = [None] * layer_count
    small_parts = [None] * layer_count
    cut = DI + STATE
    above = None
    for layer in reversed(range(layer_count)):
        below, normed, proj, raw, mixed, y, entry, extras = saved[layer]
        full_in, full_out = full[layer]
        d_branch = (valid_mask * grad_stream).astype(BF)
        keep_left, send_left = core_halves(mixed)
        keep_left, send_out = tie(keep_left, mm_tn(send_left, d_branch).astype(BF))
        d_branch, keep_out = tie(d_branch, mm_tn(keep_left, d_branch).astype(BF))
        out_parts[layer] = sum_rows(keep_out, send_out)
        d_mixed = mm_nt(d_branch, full_out).astype(BF)
        d_proj, smalls = None, None
        for seq in range(slot_count):
            if above is not None:
                d_mixed = above.advance(d_mixed)
            d_proj, smalls = mix_backward(
                proj, raw, y, entry, d_mixed, extras, seq_len, seq, d_proj, smalls
            )
        keep_left, send_left = core_halves(normed)
        if above is not None:
            send_left = above.advance(send_left)
        spans = (d_proj[:, :cut], d_proj[:, cut:])
        sends = [mm_tn(send_left, span).astype(BF) for span in spans]
        keep_left, *sends = tie(keep_left, *sends)
        keeps = [mm_tn(keep_left, span).astype(BF) for span in spans]
        if above is not None:
            in_parts[layer + 1] = above.finish()
        d_proj, *keeps = tie(d_proj, *keeps)
        above = Stages(sum_columns(keeps, sends))
        d_proj = above.advance(d_proj)
        d_hidden, d_gain = norm_back(below, norm_gain[layer], mm_nt(d_proj, full_in))
        grad_stream = grad_stream + d_hidden
        if layer > 0:
            grad_stream = above.advance(grad_stream)
        d_cw, d_cb, d_gg, d_sk, d_dtb, d_al = smalls
        d_skip = jnp.sum(d_sk.reshape(HEADS, HEAD_DIM), axis=1)
        small_parts[layer] = sum_everywhere(
            (d_gain, d_cw, d_cb[0], d_gg[0], d_dtb[0], d_al[0], d_skip)
        )
    in_parts[0] = above.finish()
    stacked = [jnp.stack([small_parts[layer][k] for layer in range(layer_count)]) for k in range(7)]
    return (
        hidden.reshape(slot_count, seq_len, width),
        grad_stream.reshape(slot_count, seq_len, width),
        jnp.stack(in_parts).astype(F32),
        jnp.stack(out_parts).astype(F32),
        *stacked,
    )


def solution(mesh):
    copies, shards = mesh.devices.shape
    mesh = Mesh(mesh.devices.reshape(copies // 2, 2, shards), ("chip", "core", "shard"))
    in_specs = (
        P(("chip", "core", "shard"), None, None),
        P(("chip", "core", "shard")),
        P(("chip", "core", "shard"), None, None),
        P(None, "shard", None),
        P(None, "shard", None),
        P(),
        P(),
        P(),
        P(),
        P(),
        P(),
        P(),
    )
    out_specs = (
        P(("chip", "core", "shard"), None, None),
        P(("chip", "core", "shard"), None, None),
        P(None, "shard", None),
        P(None, "shard", None),
        P(),
        P(),
        P(),
        P(),
        P(),
        P(),
        P(),
    )
    return jax.shard_map(
        per_device, mesh=mesh, in_specs=in_specs, out_specs=out_specs, check_vma=False
    )
```

time: 2140 us -> 803 us (0.38)
  matrix products: 669 us -> 154 us
  local copies, waits for them, and re-layouts: 424 us -> 49.2 us
  other arithmetic: 425 us -> 76 us
  waiting for transfers between devices: 516 us -> 251 us
  Pallas kernels: 0 us -> 200 us
  starting transfers between devices: 0.57 us -> 50.8 us
  blocking collectives: 43.5 us -> 0 us
  loops' own time: 34.9 us -> 0 us
    dot_general x64 -> x22, matrix products: 618 us -> 154 us  [dot_f32(): lax.dot_general(left, right, (dims, ((), ())), preferred_element_type=F32...]
    pallas_call x0 -> x6, Pallas kernels: none -> 200 us  [the longest x4 139 us: mix_backward(): pl.pallas_call(run, grid=(chunks,), in_specs=in_specs, out_specs=[at(proj...]
    mul x52 -> x0, other arithmetic: 200 us -> none  [the longest x8 83.6 us: mix_one(): act = jax.nn.silu(pre_act)]
    reduce_scatter x4 -> x2, waiting for transfers between devices: 152 us -> 10.8 us  [sum_rows(): lax.psum_scatter(part, ('shard', 'chip'), scatter_dimension=0, tiled=True)]
    psum x2 -> x0, waiting for transfers between devices: 135 us -> none  [the longest x1 115 us: per_device(): lax.psum((small_local[0], small_local[1], small_local[2], small_local[3],...]
    reshape x49 -> x6, local copies, waits for them, and re-layouts: 90.2 us -> 0.18 us  [the longest x2 0.14 us: per_device(): d_skip = jnp.sum(d_sk.reshape(HEADS, HEAD_DIM), axis=1)]
    ppermute x0 -> x40, waiting for transfers between devices: none -> 82.8 us  [the longest x14 59.8 us: flip(): lax.ppermute(value, axis, [(place, place ^ bit) for place in range(count)])]
    while x416 -> x0, local copies, waits for them, and re-layouts: 80.3 us -> none
  transfers between devices with their start and end apart: 10 -> 50, of which waited for: 6 -> 21; matrix products, arithmetic and copies ran while one was open for 46% -> 28% of each run, Pallas kernels for 0% -> 16%
where the time goes in v1:
time: 803 us; the launch traced here: 797 us
  waiting for transfers between devices  251 us (31%)
  Pallas kernels  200 us (25%)
  matrix products  154 us (19%)
  other arithmetic  76 us (9%)
  starting transfers between devices  50.8 us (6%)
  local copies, waits for them, and re-layouts  49.2 us (6%)
  between operations  16 us (2%)
    all_gather x4, waiting for transfers between devices, gather_rows(): return lax.all_gather(mine, ('shard', 'chip', 'core'), axis=0, tiled=True)  155 us
    dot_general x22, matrix products, dot_f32(): lax.dot_general(left, right, (dims, ((), ())), preferred_element_type=F32...  154 us
    pallas_call x4, Pallas kernels, mix_backward(): pl.pallas_call(run, grid=(chunks,), in_specs=in_specs, out_specs=[at(proj...  139 us
    pallas_call x2, Pallas kernels, mix_forward(): pl.pallas_call(fwd_body, grid=(seqs, chunks), in_specs=[at(proj.shape[1])...  60.7 us
    ppermute x14, waiting for transfers between devices, flip(): lax.ppermute(value, axis, [(place, place ^ bit) for place in range(count)])  59.8 us
    ppermute x26, starting transfers between devices, turn(): lax.ppermute(value, axis, [(place, (place + shift) % count) for place in...  41.8 us
    convert_element_type x14, other arithmetic, add_low(): return (left.astype(F32) + right.astype(F32)).astype(BF)  27.7 us
    unnamed x151, local copies, waits for them, and re-layouts  25 us
  transfers between devices with their start and end apart: 50, of which 21 were waited for; matrix products, arithmetic and copies ran while one was open for 28% of the time, Pallas kernels for 16%

profile of v1, /device:TPU:0, one launch (start us, length us, event | category | flops | bytes accessed | tf_op | source)
XLA Modules:
  0.0 797.5 jit_solution(15796473685408784296)
XLA Ops:
  29.6 67.9 %all-gather.21.cloned.1.call-done = bf16[1,1024,4384]{2,1,0:T(8,128)(2,1)} async-done(((bf16[1,32,4384]{2,1,0:T(8,128)(2,1)}), bf16[1,1024,4384]{2,1,0:T(8,128)(2,1)}) %all-gather.21.cloned.1.call-update) | async-done | bytes 8978448 | tf_op jit(solution)/shard_map/all_gather | solution.py:462
  99.1 15.8 %convolution_convert_fusion.1.proj_ref.refs_0_.refs_1_ = bf16[1024,4384]{1,0:T(8,128)(2,1)} fusion(bf16[1024,1024]{1,0:T(8,128)(2,1)S(1)} %multiply_convert_fusion.3, bf16[1,1024,4384]{2,1,0:T(8,128)(2,1)} %all-gather.21.cloned.1.call-done), kind=kOutput, calls=%fused_computation.1 | convolution fusion | flops 9198403584 | bytes 20054016 | tf_op jit(solution)/shard_map/dot_general | solution.py:23
  115.0 30.3 %mix_forward.2 = (bf16[1024,2048]{1,0:T(8,128)(2,1)S(1)}, bf16[1024,2048]{1,0:T(8,128)(2,1)}, bf16[8,128,2048]{2,1,0:T(8,128)(2,1)}) custom-call(bf16[1024,4384]{1,0:T(8,128)(2,1)} %convolution_convert_fusion.1.proj_ref.refs_0_.refs_1_, f32[1024,32]{1,0:T(8,128)S(1)} %fusion.63.raw_ref.refs_2_, f32[4,2304]{1,0:T(4,128)S(1)} %get-tuple-element.268.cw_ref.refs_6_, ...), custom_call_target="tpu_custom_call" | custom-call | flops 32212254720 | bytes 25165824 | tf_op jit(solution)/shard_map/mix_forward/pallas_call | solution.py:336
  147.3 14.3 %all-gather.23.cloned.1.call-done = bf16[1,2048,1024]{2,1,0:T(8,128)(2,1)} async-done(((bf16[1,64,1024]{2,1,0:T(8,128)(2,1)}), bf16[1,2048,1024]{2,1,0:T(8,128)(2,1)}) %all-gather.23.cloned.1.call-update) | async-done | bytes 4194320 | tf_op jit(solution)/shard_map/all_gather | solution.py:462
  161.6 9.3 %multiply_reduce_fusion.4 = (f32[1024]{0:T(1024)S(1)}, f32[1024,1024]{1,0:T(8,128)S(1)}) fusion(bf16[1024,2048]{1,0:T(8,128)(2,1)} %copy-done, bf16[1,2048,1024]{2,1,0:T(8,128)(2,1)} %all-gather.23.cloned.1.call-done, f32[1024]{0:T(1024)S(1)} %bitcast.210, f32[2,512,1024]{2,1,0:T(8,128)} %param.12), kind=kOutput, calls=%fused_computation.37 | convolution fusion | flops 4299160576 | bytes 16785408 | tf_op jit(solution)/shard_map/dot_general | solution.py:23
  173.3 70.4 %all-gather.25.cloned.1.call-done = bf16[1,1024,4384]{2,1,0:T(8,128)(2,1)} async-done(((bf16[1,32,4384]{2,1,0:T(8,128)(2,1)}), bf16[1,1024,4384]{2,1,0:T(8,128)(2,1)}) %all-gather.25.cloned.1.call-update) | async-done | bytes 8978448 | tf_op jit(solution)/shard_map/all_gather | solution.py:462
  245.4 15.6 %convolution_convert_fusion.proj_ref.refs_0_.refs_1_ = bf16[1024,4384]{1,0:T(8,128)(2,1)} fusion(bf16[1024,1024]{1,0:T(8,128)(2,1)S(1)} %multiply_convert_fusion.2, bf16[1,1024,4384]{2,1,0:T(8,128)(2,1)} %all-gather.25.cloned.1.call-done), kind=kOutput, calls=%fused_computation | convolution fusion | flops 9198403584 | bytes 20054016 | tf_op jit(solution)/shard_map/dot_general | solution.py:23
  261.0 30.4 %mix_forward.3 = (bf16[1024,2048]{1,0:T(8,128)(2,1)S(1)}, bf16[1024,2048]{1,0:T(8,128)(2,1)}, bf16[8,128,2048]{2,1,0:T(8,128)(2,1)}) custom-call(bf16[1024,4384]{1,0:T(8,128)(2,1)} %convolution_convert_fusion.proj_ref.refs_0_.refs_1_, f32[1024,32]{1,0:T(8,128)S(1)} %fusion.61.raw_ref.refs_2_, f32[4,2304]{1,0:T(4,128)S(1)} %get-tuple-element.267.cw_ref.refs_6_, ...), custom_call_target="tpu_custom_call" | custom-call | flops 32212254720 | bytes 25165824 | tf_op jit(solution)/shard_map/mix_forward/pallas_call | solution.py:336
  307.2 9.5 %fusion.19.refs_5_ = bf16[1024,2048]{1,0:T(8,128)(2,1)} fusion(bf16[1024,1024]{1,0:T(8,128)(2,1)} %copy-done.31, bf16[1,2048,1024]{2,1,0:T(8,128)(2,1)} %all-gather.27.cloned.1.call-done), kind=kOutput, calls=%fused_computation.49 | convolution fusion | flops 4297064448 | bytes 10485760 | tf_op jit(solution)/shard_map/dot_general | solution.py:23
  316.7 35.1 %mix_backward.4 = (bf16[1024,4384]{1,0:T(8,128)(2,1)}, f32[4,2304]{1,0:T(4,128)S(1)}, f32[1,2304]{1,0:T(1,128)S(1)}, f32[1,2048]{1,0:T(1,128)S(1)}, f32[1,2048]{...) custom-call(bf16[1024,4384]{1,0:T(8,128)(2,1)} %convolution_convert_, ...), custom_call_target="tpu_custom_call", output_to_operand_aliasing={{1}: (14, {}), {2}: (15, {}), {3}: (16, {}), {4}: (17, {}),... | custom-call | flops 37580963840 | bytes 20971520 | tf_op jit(solution)/shard_map/mix_backward/pallas_call | solution.py:408
  351.8 34.9 %mix_backward.5 = (bf16[1024,4384]{1,0:T(8,128)(2,1)}, f32[4,2304]{1,0:T(4,128)S(1)}, f32[1,2304]{1,0:T(1,128)S(1)}, f32[1,2048]{1,0:T(1,128)S(1)}, f32[1,2048]{...) custom-call(bf16[1024,4384]{1,0:T(8,128)(2,1)} %convolution_convert_, ...), custom_call_target="tpu_custom_call", output_to_operand_aliasing={{1}: (14, {}), {2}: (15, {}), {3}: (16, {}), {4}: (17, {}),... | custom-call | flops 37580963840 | bytes 20971520 | tf_op jit(solution)/shard_map/mix_backward/pallas_call | solution.py:408
  386.7 6.7 convolution_convert_fusion.9
  440.7 17.4 %multiply_reduce_fusion = (f32[1024]{0:T(1024)S(1)}, f32[1024]{0:T(1024)S(1)}, f32[1024,1024]{1,0:T(8,128)}) fusion(f32[1024,1024]{1,0:T(8,128)} %copy-done.22, f32[1024]{0:T(1024)S(1)} %copy-done.55, f32[1024]{0:T(1024)S(1)} %bitcast.206, bf16[1024,4384]{1,0:T(8,128)(2,1)} %get-tuple-element.127, bf16[1,1024,4384]{2,1,0:T(8,128)(2,1)} %all-gather.25.cloned.1.call-done), kind=kOutput, calls=%fused_computation.25 | convolution fusion | flops 9200203776 | bytes 26361856 | tf_op jit(solution)/shard_map/dot_general | solution.py:23
  467.5 8.3 %collective-permute-done.2 = bf16[4,1,2,32,2176]{4,3,2,1,0:T(8,128)(2,1)} collective-permute-done((bf16[4,1,2,32,2176]{4,3,2,1,0:T(8,128)(2,1)}, bf16[4,1,2,32,2176]{4,3,2,1,0:T(8,128)(2,1)}, u32[]{:S(2)}, u32[]{:S(2)}) %collective-permute-start.2) | collective-permute-done | bytes 1114144 | tf_op jit(solution)/shard_map/ppermute | solution.py:467
  475.8 17.7 %collective-permute-done.3 = bf16[4,2,1,32,2208]{4,3,2,1,0:T(8,128)(2,1)} collective-permute-done((bf16[4,2,1,32,2208]{4,3,2,1,0:T(8,128)(2,1)}, bf16[4,2,1,32,2208]{4,3,2,1,0:T(8,128)(2,1)}, u32[]{:S(2)}, u32[]{:S(2)}) %collective-permute-start.3) | collective-permute-done | bytes 1130528 | tf_op jit(solution)/shard_map/ppermute | solution.py:467
  539.8 34.7 %mix_backward.6 = (bf16[1024,4384]{1,0:T(8,128)(2,1)}, f32[4,2304]{1,0:T(4,128)S(1)}, f32[1,2304]{1,0:T(1,128)S(1)}, f32[1,2048]{1,0:T(1,128)S(1)}, f32[1,2048]{...) custom-call(bf16[1024,4384]{1,0:T(8,128)(2,1)} %convolution_convert_, ...), custom_call_target="tpu_custom_call", output_to_operand_aliasing={{1}: (14, {}), {2}: (15, {}), {3}: (16, {}), {4}: (17, {}),... | custom-call | flops 37580963840 | bytes 20971520 | tf_op jit(solution)/shard_map/mix_backward/pallas_call | solution.py:408
  581.4 34.7 %mix_backward.7 = (bf16[1024,4384]{1,0:T(8,128)(2,1)}, f32[4,2304]{1,0:T(4,128)S(1)}, f32[1,2304]{1,0:T(1,128)S(1)}, f32[1,2048]{1,0:T(1,128)S(1)}, f32[1,2048]{...) custom-call(bf16[1024,4384]{1,0:T(8,128)(2,1)} %convolution_convert_, ...), custom_call_target="tpu_custom_call", output_to_operand_aliasing={{1}: (14, {}), {2}: (15, {}), {3}: (16, {}), {4}: (17, {}),... | custom-call | flops 37580963840 | bytes 20971520 | tf_op jit(solution)/shard_map/mix_backward/pallas_call | solution.py:408
  632.0 6.7 convolution_convert_fusion.3
  649.4 10.8 %reduce-scatter.3.cloned.1.call-done = bf16[64,1024]{1,0:T(8,128)(2,1)} async-done(((bf16[1024,1024]{1,0:T(8,128)(2,1)}), bf16[64,1024]{1,0:T(8,128)(2,1)}) %reduce-scatter.3.cloned.1.call-update) | async-done | bytes 131088 | tf_op jit(solution)/shard_map/reduce_scatter | solution.py:574
  666.5 19.3 %collective-permute-done.14 = bf16[4,1,2,32,2176]{4,3,2,1,0:T(8,128)(2,1)} collective-permute-done((bf16[4,1,2,32,2176]{4,3,2,1,0:T(8,128)(2,1)}, bf16[4,1,2,32,2176]{4,3,2,1,0:T(8,128)(2,1)}, u32[]{:S(2)}, u32[]{:S(2)}) %collective-permute-start.14) | collective-permute-done | bytes 1114144 | tf_op jit(solution)/shard_map/ppermute | solution.py:467
  725.6 17.6 %multiply_reduce_fusion.1 = (f32[1024]{0:T(1024)S(1)}, f32[1024]{0:T(1024)S(1)}, f32[1024,1024]{1,0:T(8,128)}) fusion(f32[2,512,1024]{2,1,0:T(8,128)} %param.12, f32[1024]{0:T(1024)S(1)} %bitcast.200, f32[1024]{0:T(1024)S(1)} %bitcast.203, bf16[1024,4384]{1,0:T(8,128)(2,1)} %get-tuple-element.168, bf16[1,1024,4384]{2,1,0:T(8,128)(2,1)} %all-gather.21.cloned.1.call-done), kind=kOutput, calls=%fused_computation.26 | convolution fusion | flops 9200203776 | bytes 26361856 | tf_op jit(solution)/shard_map/dot_general | solution.py:23
  757.1 7.1 multiply_add_fusion
  774.5 6.5 maximum_convert_fusion
  781.1 9.3 %copy.88 = f32[2,256,4384]{1,2,0:T(8,128)} copy(f32[2,256,4384]{2,1,0:T(8,128)} %maximum_convert_fusion) | data formatting | bytes 17956864
  (391 shorter events, 251.1 us)
Async XLA Ops:
  7.2 90.3 %all-gather.21.cloned.1.call-start = ((), (), s32[]{:S(2)}) async-start(), calls=%async_computation.8 | async-start | bytes 9461760 | tf_op jit(solution)/shard_map/all_gather | solution.py:462
  13.9 147.7 %all-gather.23.cloned.1.call-start = ((), (), s32[]{:S(2)}) async-start(), calls=%async_computation.9 | async-start | bytes 4325376 | tf_op jit(solution)/shard_map/all_gather | solution.py:462
  17.3 226.4 %all-gather.25.cloned.1.call-start = ((), (), s32[]{:S(2)}) async-start(), calls=%async_computation.10 | async-start | bytes 9461760 | tf_op jit(solution)/shard_map/all_gather | solution.py:462
  18.9 288.3 %all-gather.27.cloned.1.call-start = ((), (), s32[]{:S(2)}) async-start(), calls=%async_computation.11 | async-start | bytes 4325376 | tf_op jit(solution)/shard_map/all_gather | solution.py:462
  20.5 611.4 %reduce-scatter.5.cloned.1.call-start = ((), (), s32[]{:S(2)}) async-start(), calls=%async_computation.6 | async-start | bytes 2228224 | tf_op jit(solution)/shard_map/reduce_scatter | solution.py:574
  425.4 234.8 %reduce-scatter.3.cloned.1.call-start = ((), (), s32[]{:S(2)}) async-start(), calls=%async_computation.4 | async-start | bytes 2228224 | tf_op jit(solution)/shard_map/reduce_scatter | solution.py:574
  438.6 37.2 %collective-permute-start.2 = (bf16[4,1,2,32,2176]{4,3,2,1,0:T(8,128)(2,1)}, bf16[4,1,2,32,2176]{4,3,2,1,0:T(8,128)(2,1)}, u32[]{:S(2)}, u32[]{:S(2)}) collective-permute-start(bf16[4,1,2,32,2176]{4,3,2,1,0:T(8,128)(2,1)} %constant_dynamic-slice_fusion.7), channel_id=1, source_target_pairs={{0,16},{8,24},{16,0},{24,8},{1,17},{9,25},{17,1},{25,9},{2,18},{10... | collective-permute-start | bytes 3342344 | tf_op jit(solution)/shard_map/ppermute | solution.py:467
  440.1 53.4 %collective-permute-start.3 = (bf16[4,2,1,32,2208]{4,3,2,1,0:T(8,128)(2,1)}, bf16[4,2,1,32,2208]{4,3,2,1,0:T(8,128)(2,1)}, u32[]{:S(2)}, u32[]{:S(2)}) collective-permute-start(bf16[4,2,1,32,2208]{4,3,2,1,0:T(8,128)(2,1)} %constant_dynamic-slice_fusion.6), channel_id=1, source_target_pairs={{0,8},{8,0},{16,24},{24,16},{1,9},{9,1},{17,25},{25,17},{2,10},{10... | collective-permute-start | bytes 3391496 | tf_op jit(solution)/shard_map/ppermute | solution.py:467
  463.7 57.0 %collective-permute-start.35 = (f32[120,128]{1,0:T(8,128)S(1)}, f32[120,128]{1,0:T(8,128)S(1)}, u32[]{:S(2)}, u32[]{:S(2)}) collective-permute-start(f32[120,128]{1,0:T(8,128)S(1)} %fusion.82), channel_id=1, source_target_pairs={{0,16},{8,24},{16,0},{24,8},{1,17},{9,25},{17,1},{25,9},{2,18},{10... | collective-permute-start | bytes 184328 | tf_op jit(solution)/shard_map/ppermute | solution.py:472
  465.0 55.7 %collective-permute-start.36 = (f32[120,128]{1,0:T(8,128)S(1)}, f32[120,128]{1,0:T(8,128)S(1)}, u32[]{:S(2)}, u32[]{:S(2)}) collective-permute-start(f32[120,128]{1,0:T(8,128)S(1)} %fusion.82), channel_id=1, source_target_pairs={{0,24},{8,0},{16,8},{24,16},{1,25},{9,1},{17,9},{25,17},{2,26},{10... | collective-permute-start | bytes 184328 | tf_op jit(solution)/shard_map/ppermute | solution.py:472
  466.8 53.9 %collective-permute-start.34 = (f32[120,128]{1,0:T(8,128)S(1)}, f32[120,128]{1,0:T(8,128)S(1)}, u32[]{:S(2)}, u32[]{:S(2)}) collective-permute-start(f32[120,128]{1,0:T(8,128)S(1)} %fusion.82), channel_id=1, source_target_pairs={{0,8},{8,16},{16,24},{24,0},{1,9},{9,17},{17,25},{25,1},{2,10},{10... | collective-permute-start | bytes 184328 | tf_op jit(solution)/shard_map/ppermute | solution.py:472
  520.7 55.9 %collective-permute-start.24 = (bf16[1024,1024]{1,0:T(8,128)(2,1)}, bf16[1024,1024]{1,0:T(8,128)(2,1)S(1)}, u32[]{:S(2)}, u32[]{:S(2)}) collective-permute-start(bf16[1024,1024]{1,0:T(8,128)(2,1)} %fusion.42), channel_id=1, source_target_pairs={{0,4},{4,0},{1,5},{5,1},{2,6},{6,2},{3,7},{7,3},{8,12},{12,8},{9,1... | collective-permute-start | bytes 6291464 | tf_op jit(solution)/shard_map/ppermute | solution.py:467
  520.8 53.7 %collective-permute-start.8 = (bf16[32,2176]{1,0:T(8,128)(2,1)S(1)}, bf16[32,2176]{1,0:T(8,128)(2,1)S(1)}, u32[]{:S(2)}, u32[]{:S(2)}) collective-permute-start(bf16[32,2176]{1,0:T(8,128)(2,1)S(1)} %get-tuple-element.146), channel_id=1, source_target_pairs={{0,3},{1,0},{2,1},{3,2},{4,7},{5,4},{6,5},{7,6},{8,11},{9,8},{10,9... | collective-permute-start | bytes 417800 | tf_op jit(solution)/shard_map/ppermute | solution.py:472
  522.1 52.5 %collective-permute-start.9 = (bf16[32,2208]{1,0:T(8,128)(2,1)S(1)}, bf16[32,2208]{1,0:T(8,128)(2,1)S(1)}, u32[]{:S(2)}, u32[]{:S(2)}) collective-permute-start(bf16[32,2208]{1,0:T(8,128)(2,1)S(1)} %get-tuple-element.147), channel_id=1, source_target_pairs={{0,1},{1,2},{2,3},{3,0},{4,5},{5,6},{6,7},{7,4},{8,9},{9,10},{10,1... | collective-permute-start | bytes 423944 | tf_op jit(solution)/shard_map/ppermute | solution.py:472
  526.3 48.4 %collective-permute-start.10 = (bf16[32,2208]{1,0:T(8,128)(2,1)S(1)}, bf16[32,2208]{1,0:T(8,128)(2,1)S(1)}, u32[]{:S(2)}, u32[]{:S(2)}) collective-permute-start(bf16[32,2208]{1,0:T(8,128)(2,1)S(1)} %get-tuple-element.148), channel_id=1, source_target_pairs={{0,2},{1,3},{2,0},{3,1},{4,6},{5,7},{6,4},{7,5},{8,10},{9,11},{10,... | collective-permute-start | bytes 423944 | tf_op jit(solution)/shard_map/ppermute | solution.py:472
  535.5 41.1 %collective-permute-start.11 = (bf16[32,2208]{1,0:T(8,128)(2,1)S(1)}, bf16[32,2208]{1,0:T(8,128)(2,1)S(1)}, u32[]{:S(2)}, u32[]{:S(2)}) collective-permute-start(bf16[32,2208]{1,0:T(8,128)(2,1)S(1)} %get-tuple-element.149), channel_id=1, source_target_pairs={{0,3},{1,0},{2,1},{3,2},{4,7},{5,4},{6,5},{7,6},{8,11},{9,8},{10,9... | collective-permute-start | bytes 423944 | tf_op jit(solution)/shard_map/ppermute | solution.py:472
  574.5 53.2 %collective-permute-start.39 = (f32[120,128]{1,0:T(8,128)S(1)}, f32[120,128]{1,0:T(8,128)S(1)}, u32[]{:S(2)}, u32[]{:S(2)}) collective-permute-start(f32[120,128]{1,0:T(8,128)S(1)} %add_add_fusion.1), channel_id=1, source_target_pairs={{0,3},{1,0},{2,1},{3,2},{4,7},{5,4},{6,5},{7,6},{8,11},{9,8},{10,9... | collective-permute-start | bytes 184328 | tf_op jit(solution)/shard_map/ppermute | solution.py:472
  574.6 53.1 %collective-permute-start.38 = (f32[120,128]{1,0:T(8,128)S(1)}, f32[120,128]{1,0:T(8,128)S(1)}, u32[]{:S(2)}, u32[]{:S(2)}) collective-permute-start(f32[120,128]{1,0:T(8,128)S(1)} %add_add_fusion.1), channel_id=1, source_target_pairs={{0,2},{1,3},{2,0},{3,1},{4,6},{5,7},{6,4},{7,5},{8,10},{9,11},{10,... | collective-permute-start | bytes 184328 | tf_op jit(solution)/shard_map/ppermute | solution.py:472
  574.7 53.1 %collective-permute-start.37 = (f32[120,128]{1,0:T(8,128)S(1)}, f32[120,128]{1,0:T(8,128)S(1)}, u32[]{:S(2)}, u32[]{:S(2)}) collective-permute-start(f32[120,128]{1,0:T(8,128)S(1)} %add_add_fusion.1), channel_id=1, source_target_pairs={{0,1},{1,2},{2,3},{3,0},{4,5},{5,6},{6,7},{7,4},{8,9},{9,10},{10,1... | collective-permute-start | bytes 184328 | tf_op jit(solution)/shard_map/ppermute | solution.py:472
  579.0 189.6 %all-gather.19.cloned.1.call-start = ((), (), s32[]{:S(2)}) async-start(), calls=%async_computation.7 | async-start | bytes 1179648 | tf_op jit(solution)/shard_map/all_gather | solution.py:575
  631.9 136.7 %all-gather.17.cloned.1.call-start = ((), (), s32[]{:S(2)}) async-start(), calls=%async_computation.5 | async-start | bytes 1179648 | tf_op jit(solution)/shard_map/all_gather | solution.py:575
  660.2 112.2 %all-gather.15.cloned.1.call-start = ((), (), s32[]{:S(2)}) async-start(), calls=%async_computation.3 | async-start | bytes 2580480 | tf_op jit(solution)/shard_map/all_gather | solution.py:569
  664.7 28.8 %collective-permute-start.19 = (bf16[4,2,1,32,2208]{4,3,2,1,0:T(8,128)(2,1)}, bf16[4,2,1,32,2208]{4,3,2,1,0:T(8,128)(2,1)}, u32[]{:S(2)}, u32[]{:S(2)}) collective-permute-start(bf16[4,2,1,32,2208]{4,3,2,1,0:T(8,128)(2,1)} %constant_dynamic-slice_fusion.2), channel_id=1, source_target_pairs={{0,8},{8,0},{16,24},{24,16},{1,9},{9,1},{17,25},{25,17},{2,10},{10... | collective-permute-start | bytes 3391496 | tf_op jit(solution)/shard_map/ppermute | solution.py:467
  666.4 108.2 %all-gather.13.cloned.1.call-start = ((), (), s32[]{:S(2)}) async-start(), calls=%async_computation.2 | async-start | bytes 2580480 | tf_op jit(solution)/shard_map/all_gather | solution.py:569
  (97 other events, 1843.5 us)
Sparse Core Ops, SparseCore 0:
  14.0 83.3 all-gather.20
  100.9 60.6 all-gather.22
  164.5 79.2 all-gather.24
  246.4 60.6 all-gather.26
  425.5 87.0 reduce-scatter.4
  579.1 81.0 reduce-scatter.2
  662.1 25.1 all-gather.18
  689.1 24.2 all-gather.16
  715.3 28.7 all-gather.14
  745.8 28.7 all-gather.12

commit v2 on v1

--- a/solution.py
+++ b/solution.py
@@ -428,13 +428,102 @@
             dimension_semantics=("arbitrary",), vmem_limit_bytes=48 << 20
         ),
         cost_estimate=pl.CostEstimate(
-            flops=70 * seq_len * DI * 512,
-            bytes_accessed=seq_len * 40 * 1024,
-            transcendentals=seq_len * DI,
+            flops=seq_len * DI * 512,
+            bytes_accessed=seq_len * 10 * 1024,
+            transcendentals=seq_len,
         ),
         name="mix_backward",
     )(*operands)
     return d_proj, sums
+
+
+def assemble_body(place, low_own, low_far, high_own, high_far, out_ref):
+    chips = low_own.shape[0]
+    rows = low_own.shape[2]
+    cut = low_own.shape[3]
+    own = pl.program_id(1) == place[0]
+    for chip in range(chips):
+        far = chip ^ place[1]
+        turned = 0
+        for bit in range(chips.bit_length() - 1):
+            turned = 2 * turned + (far // (1 << bit)) % 2
+        span = slice(chip * rows, (chip + 1) * rows)
+
+        @pl.when(own)
+        def _():
+            out_ref[span, :cut] = low_own[far, 0]
+            out_ref[span, cut:] = high_own[turned, 0]
+
+        @pl.when(jnp.logical_not(own))
+        def _():
+            out_ref[span, :cut] = low_far[far, 0]
+            out_ref[span, cut:] = high_far[turned, 0]
+
+
+def assemble(place, low_own, low_far, high_own, high_far):
+    chips, shards, rows, cut = low_own.shape
+    rest = high_own.shape[3]
+
+    def blocks(width):
+        return pl.BlockSpec(
+            (chips, 1, rows, width),
+            lambda shard, core, place: (0, (place[2] - shard + shards) % shards, 0, 0),
+        )
+
+    return pl.pallas_call(
+        assemble_body,
+        grid_spec=pltpu.PrefetchScalarGridSpec(
+            num_scalar_prefetch=1,
+            grid=(shards, 2),
+            in_specs=[blocks(cut), blocks(cut), blocks(rest), blocks(rest)],
+            out_specs=pl.BlockSpec(
+                (chips * rows, cut + rest), lambda shard, core, place: (2 * shard + core, 0)
+            ),
+        ),
+        out_shape=jax.ShapeDtypeStruct((shards * 2 * chips * rows, cut + rest), low_own.dtype),
+        compiler_params=pltpu.CompilerParams(
+            dimension_semantics=("arbitrary", "arbitrary"), vmem_limit_bytes=48 << 20
+        ),
+        name="assemble",
+    )(place, low_own, low_far, high_own, high_far)
+
+
+def widen_body(low_ref, *refs):
+    refs[-1][0] = low_ref[...].astype(F32)
+
+
+def widen_turned_body(low_ref, *refs):
+    for start in range(0, low_ref.shape[1], 128):
+        stop = min(start + 128, low_ref.shape[1])
+        refs[-1][0, start:stop, :] = low_ref[:, start:stop].astype(F32).T
+
+
+def widen(low, layer, layers, earlier, turned):
+    rows, width = low.shape
+    tile = min(rows, 128)
+    operands, specs, aliases = [low], [pl.BlockSpec((tile, width), lambda k: (k, 0))], {}
+    if earlier is not None:
+        operands.append(earlier)
+        specs.append(pl.BlockSpec(memory_space=pl.ANY))
+        aliases = {1: 0}
+    if turned:
+        shape = (layers, width, rows)
+        out_spec = pl.BlockSpec((1, width, tile), lambda k: (layer, 0, k))
+    else:
+        shape = (layers, rows, width)
+        out_spec = pl.BlockSpec((1, tile, width), lambda k: (layer, k, 0))
+    return pl.pallas_call(
+        widen_turned_body if turned else widen_body,
+        grid=(rows // tile,),
+        in_specs=specs,
+        out_specs=out_spec,
+        out_shape=jax.ShapeDtypeStruct(shape, F32),
+        input_output_aliases=aliases,
+        compiler_params=pltpu.CompilerParams(
+            dimension_semantics=("arbitrary",), vmem_limit_bytes=48 << 20
+        ),
+        name="widen",
+    )(*operands)
 
 
 def rms_scale(values, gain):
@@ -569,10 +658,32 @@
     return lax.all_gather(owned, ("core", "chip"), axis=0, tiled=True)
 
 
-def sum_rows(keep, send):
-    part = add_low(keep, flip(send, "core"))
-    owned = lax.psum_scatter(part, ("shard", "chip"), scatter_dimension=0, tiled=True)
-    return lax.all_gather(owned, ("core", "chip"), axis=0, tiled=True)
+def gather_in_stages(shard_rows, cut):
+    chips = lax.axis_size("chip")
+    core, chip, shard = (lax.axis_index(axis) for axis in ("core", "chip", "shard"))
+    count = shard_rows.shape[0] // (2 * chips)
+    mine = lax.dynamic_slice_in_dim(shard_rows, (core * chips + chip) * count, count, 0)
+    others = [turn(mine, "shard", shift) for shift in range(1, lax.axis_size("shard"))]
+    line = jnp.stack([mine] + others)[None]
+    bits = [1 << k for k in range(chips.bit_length() - 1)]
+    spans = [line[..., :cut], line[..., cut:]]
+    orders = (bits, bits[::-1])
+    near = []
+    for step in range(len(bits)):
+        spans = [(span, flip(span, "chip", order[step])) for span, order in zip(spans, orders)]
+        spans = [jnp.concatenate(pair, axis=0) for pair in spans]
+    low, high = spans
+    far = [flip(span, "core") for span in (low, high)]
+    place = jnp.stack([core, chip, shard]).astype(jnp.int32)
+    return assemble(place, low, far[0], high, far[1])
+
+
+def sum_rows(part):
+    axes = ("shard", "chip")
+    ready = yield [lax.psum_scatter(part, axes, scatter_dimension=0, tiled=True)]
+    ready = yield ready
+    arrived = yield [lax.all_gather(ready[0], ("core", "chip"), axis=0, tiled=True)]
+    return arrived[0]
 
 
 def sum_everywhere(values):
@@ -610,36 +721,40 @@
     valid_mask = (places < lengths[:, None]).astype(F32).reshape(row_total, 1)
     layer_count = w_in.shape[0]
     raw_start = 2 * DI + 2 * STATE
-    full = [(gather_rows(w_in[layer]), gather_rows(w_out[layer])) for layer in range(layer_count)]
+    all_in = [gather_rows(w_in[layer]) for layer in range(layer_count)]
+    all_out = [gather_in_stages(w_out[0], width // 2)]
+    all_in[0], all_out[0] = tie(all_in[0], all_out[0])
     hidden = inputs.reshape(row_total, width)
     saved = []
     for layer in range(layer_count):
-        full_in, full_out = full[layer]
+        full_in, full_out = all_in[layer], all_out[layer]
         extras = tuple(
             item[layer] for item in (conv_weight, conv_bias, gate_gain, dt_bias, a_log, skip)
         )
         normed = rms_scale(hidden, norm_gain[layer]).astype(BF)
         proj = mm(normed, full_in).astype(BF)
         raw = mm(normed, full_in[:, raw_start:])
+        if layer + 1 < layer_count:
+            proj, rows_next = tie(proj, w_out[layer + 1])
+            all_out.append(gather_rows(rows_next))
         mixed, y, entry = mix_forward(proj, raw, extras, seq_len)
         saved.append((hidden, normed, proj, raw, mixed, y, entry, extras))
         hidden = hidden + valid_mask * mm(mixed, full_out)
     grad_stream = cotangent.reshape(row_total, width)
-    grad_stream, mixed_last = tie(grad_stream, saved[-1][4])
-    saved[-1] = saved[-1][:4] + (mixed_last,) + saved[-1][5:]
-    in_parts = [None] * layer_count
-    out_parts = [None] * layer_count
+    grad_in, grad_out = None, None
     small_parts = [None] * layer_count
     cut = DI + STATE
     above = None
     for layer in reversed(range(layer_count)):
         below, normed, proj, raw, mixed, y, entry, extras = saved[layer]
-        full_in, full_out = full[layer]
+        full_in, full_out = all_in[layer], all_out[layer]
         d_branch = (valid_mask * grad_stream).astype(BF)
         keep_left, send_left = core_halves(mixed)
         keep_left, send_out = tie(keep_left, mm_tn(send_left, d_branch).astype(BF))
-        d_branch, keep_out = tie(d_branch, mm_tn(keep_left, d_branch).astype(BF))
-        out_parts[layer] = sum_rows(keep_out, send_out)
+        keep_out = mm_tn(keep_left, d_branch).astype(BF)
+        part_out = add_low(keep_out, flip(send_out, "core"))
+        d_branch, part_out, full_out = tie(d_branch, part_out, full_out)
+        beside = Stages(sum_rows(part_out))
         d_mixed = mm_nt(d_branch, full_out).astype(BF)
         d_proj, smalls = None, None
         for seq in range(slot_count):
@@ -651,31 +766,37 @@
         keep_left, send_left = core_halves(normed)
         if above is not None:
             send_left = above.advance(send_left)
+        send_left = beside.advance(send_left)
         spans = (d_proj[:, :cut], d_proj[:, cut:])
         sends = [mm_tn(send_left, span).astype(BF) for span in spans]
         keep_left, *sends = tie(keep_left, *sends)
         keeps = [mm_tn(keep_left, span).astype(BF) for span in spans]
         if above is not None:
-            in_parts[layer + 1] = above.finish()
+            grad_in = widen(above.finish(), layer + 1, layer_count, grad_in, True)
         d_proj, *keeps = tie(d_proj, *keeps)
         above = Stages(sum_columns(keeps, sends))
         d_proj = above.advance(d_proj)
-        d_hidden, d_gain = norm_back(below, norm_gain[layer], mm_nt(d_proj, full_in))
+        d_normed = mm_nt(d_proj, full_in)
+        if layer == 0:
+            d_normed = above.advance(d_normed)
+        d_hidden, d_gain = norm_back(below, norm_gain[layer], d_normed)
         grad_stream = grad_stream + d_hidden
+        grad_stream = above.advance(grad_stream)
         if layer > 0:
-            grad_stream = above.advance(grad_stream)
+            grad_stream = beside.advance(grad_stream)
+        grad_out = widen(beside.finish(), layer, layer_count, grad_out, False)
         d_cw, d_cb, d_gg, d_sk, d_dtb, d_al = smalls
         d_skip = jnp.sum(d_sk.reshape(HEADS, HEAD_DIM), axis=1)
         small_parts[layer] = sum_everywhere(
             (d_gain, d_cw, d_cb[0], d_gg[0], d_dtb[0], d_al[0], d_skip)
         )
-    in_parts[0] = above.finish()
+    grad_in = widen(above.finish(), 0, layer_count, grad_in, True)
     stacked = [jnp.stack([small_parts[layer][k] for layer in range(layer_count)]) for k in range(7)]
     return (
         hidden.reshape(slot_count, seq_len, width),
         grad_stream.reshape(slot_count, seq_len, width),
-        jnp.stack(in_parts).astype(F32),
-        jnp.stack(out_parts).astype(F32),
+        jnp.swapaxes(grad_in, 1, 2),
+        grad_out,
         *stacked,
     )
 

time: 803 us -> 716 us (0.89)
  waiting for transfers between devices: 251 us -> 155 us
  Pallas kernels: 200 us -> 214 us
  other arithmetic: 76 us -> 63.3 us
  starting transfers between devices: 50.8 us -> 62.1 us
    all_gather x4 -> x3, waiting for transfers between devices: 155 us -> 58.8 us  [gather_rows(): return lax.all_gather(mine, ('shard', 'chip', 'core'), axis=0, tiled=True)]
    pallas_call x0 -> x5, Pallas kernels: none -> 13.4 us  [the longest x4 8.64 us: widen(): pl.pallas_call(widen_turned_body if turned else widen_body, grid=(rows //...]
    convert_element_type x14 -> x12, other arithmetic: 27.7 us -> 16.4 us  [add_low(): return (left.astype(F32) + right.astype(F32)).astype(BF)]
    convert_element_type x2 -> x0, other arithmetic: 10.4 us -> none  [the longest x1 6.55 us: per_device(): jnp.stack(in_parts).astype(F32)]
    reduce_scatter x2, waiting for transfers between devices: 10.8 us -> 1.49 us  [sum_rows(): lax.psum_scatter(part, axes, scatter_dimension=0, tiled=True)]
    ppermute x26 -> x29, waiting for transfers between devices: 23.1 us -> 31.3 us  [turn(): lax.ppermute(value, axis, [(place, (place + shift) % count) for place in...]
    ppermute x14 -> x20, starting transfers between devices: 8.34 us -> 16.5 us  [flip(): lax.ppermute(value, axis, [(place, place ^ bit) for place in range(count)])]
    unnamed x151 -> x152, local copies, waits for them, and re-layouts: 25 us -> 17.8 us
  transfers between devices with their start and end apart: 50 -> 58, of which waited for: 21 -> 30; matrix products, arithmetic and copies ran while one was open for 28% -> 31% of each run, Pallas kernels for 16% -> 30%
where the time goes in v2:
time: 716 us; the launch traced here: 711 us
  Pallas kernels  214 us (30%)
  matrix products  159 us (22%)
  waiting for transfers between devices  155 us (22%)
  other arithmetic  63.3 us (9%)
  starting transfers between devices  62.1 us (9%)
  local copies, waits for them, and re-layouts  42.6 us (6%)
  between operations  15.6 us (2%)
    dot_general x22, matrix products, dot_f32(): lax.dot_general(left, right, (dims, ((), ())), preferred_element_type=F32...  159 us
    pallas_call x4, Pallas kernels, mix_backward(): pl.pallas_call(run, grid=(chunks,), in_specs=in_specs, out_specs=[at(proj...  140 us
    ppermute x20, waiting for transfers between devices, flip(): lax.ppermute(value, axis, [(place, place ^ bit) for place in range(count)])  63.4 us
    pallas_call x2, Pallas kernels, mix_forward(): pl.pallas_call(fwd_body, grid=(seqs, chunks), in_specs=[at(proj.shape[1])...  60.8 us
    all_gather x3, waiting for transfers between devices, gather_rows(): return lax.all_gather(mine, ('shard', 'chip', 'core'), axis=0, tiled=True)  58.8 us
    ppermute x29, starting transfers between devices, turn(): lax.ppermute(value, axis, [(place, (place + shift) % count) for place in...  44.9 us
    ppermute x29, waiting for transfers between devices, turn(): lax.ppermute(value, axis, [(place, (place + shift) % count) for place in...  31.3 us
    unnamed x152, local copies, waits for them, and re-layouts  17.8 us
  transfers between devices with their start and end apart: 58, of which 30 were waited for; matrix products, arithmetic and copies ran while one was open for 31% of the time, Pallas kernels for 30%

profile of v2, /device:TPU:0, one launch (start us, length us, event | category | flops | bytes accessed | tf_op | source)
XLA Modules:
  0.0 711.3 jit_solution(3762289390674218925)
XLA Ops:
  28.8 11.1 %collective-permute-done.1 = bf16[64,1024]{1,0:T(8,128)(2,1)S(1)} collective-permute-done((bf16[64,1024]{1,0:T(8,128)(2,1)S(1)}, bf16[64,1024]{1,0:T(8,128)(2,1)S(1)}, u32[]{:S(2)}, u32[]{:S(2)}) %collective-permute-start.1) | collective-permute-done | bytes 131104 | tf_op jit(solution)/shard_map/ppermute | solution.py:561
  54.4 9.1 %collective-permute-done.4 = bf16[2,4,64,512]{3,2,1,0:T(8,128)(2,1)} collective-permute-done((bf16[2,4,64,512]{3,2,1,0:T(8,128)(2,1)}, bf16[2,4,64,512]{3,2,1,0:T(8,128)(2,1)}, u32[]{:S(2)}, u32[]{:S(2)}) %collective-permute-start.4) | collective-permute-done | bytes 524320 | tf_op jit(solution)/shard_map/ppermute | solution.py:556
  76.5 33.3 %all-gather.20.cloned.1.call-done = bf16[1,1024,4384]{2,1,0:T(8,128)(2,1)} async-done(((bf16[1,32,4384]{2,1,0:T(8,128)(2,1)}), bf16[1,1024,4384]{2,1,0:T(8,128)(2,1)}) %all-gather.20.cloned.1.call-update) | async-done | bytes 8978448 | tf_op jit(solution)/shard_map/all_gather | solution.py:551
  109.8 15.6 %convolution_convert_fusion.1.proj_ref.refs_0_.refs_1_ = bf16[1024,4384]{1,0:T(8,128)(2,1)} fusion(bf16[1024,1024]{1,0:T(8,128)(2,1)S(1)} %multiply_convert_fusion.2, bf16[1024,4384]{1,0:T(8,128)(2,1)} %bitcast.213), kind=kOutput, calls=%fused_computation.1 | convolution fusion | flops 9198403584 | bytes 20054016 | tf_op jit(solution)/shard_map/dot_general | solution.py:23
  128.7 30.5 %mix_forward.2 = (bf16[1024,2048]{1,0:T(8,128)(2,1)S(1)}, bf16[1024,2048]{1,0:T(8,128)(2,1)}, bf16[8,128,2048]{2,1,0:T(8,128)(2,1)}) custom-call(bf16[1024,4384]{1,0:T(8,128)(2,1)} %convolution_convert_fusion.1.proj_ref.refs_0_.refs_1_, f32[1024,32]{1,0:T(8,128)S(1)} %fusion.46.raw_ref.refs_2_, f32[4,2304]{1,0:T(4,128)S(1)} %get-tuple-element.300.cw_ref.refs_6_, ...), custom_call_target="tpu_custom_call" | custom-call | flops 32212254720 | bytes 25165824 | tf_op jit(solution)/shard_map/mix_forward/pallas_call | solution.py:336
  159.3 6.4 multiply_reduce_fusion.4
  168.7 23.4 %all-gather.22.cloned.1.call-done = bf16[1,1024,4384]{2,1,0:T(8,128)(2,1)} async-done(((bf16[1,32,4384]{2,1,0:T(8,128)(2,1)}), bf16[1,1024,4384]{2,1,0:T(8,128)(2,1)}) %all-gather.22.cloned.1.call-update) | async-done | bytes 8978448 | tf_op jit(solution)/shard_map/all_gather | solution.py:551
  193.7 15.6 %convolution_convert_fusion.proj_ref.refs_0_.refs_1_ = bf16[1024,4384]{1,0:T(8,128)(2,1)} fusion(bf16[1024,1024]{1,0:T(8,128)(2,1)S(1)} %multiply_convert_fusion.1, bf16[1,1024,4384]{2,1,0:T(8,128)(2,1)} %all-gather.22.cloned.1.call-done), kind=kOutput, calls=%fused_computation | convolution fusion | flops 9198403584 | bytes 20054016 | tf_op jit(solution)/shard_map/dot_general | solution.py:23
  209.3 30.3 %mix_forward.3 = (bf16[1024,2048]{1,0:T(8,128)(2,1)S(1)}, bf16[1024,2048]{1,0:T(8,128)(2,1)}, bf16[8,128,2048]{2,1,0:T(8,128)(2,1)}) custom-call(bf16[1024,4384]{1,0:T(8,128)(2,1)} %convolution_convert_fusion.proj_ref.refs_0_.refs_1_, f32[1024,32]{1,0:T(8,128)S(1)} %fusion.44.raw_ref.refs_2_, f32[4,2304]{1,0:T(4,128)S(1)} %get-tuple-element.299.cw_ref.refs_6_, ...), custom_call_target="tpu_custom_call" | custom-call | flops 32212254720 | bytes 25165824 | tf_op jit(solution)/shard_map/mix_forward/pallas_call | solution.py:336
  265.6 34.6 %mix_backward.4 = (bf16[1024,4384]{1,0:T(8,128)(2,1)}, f32[4,2304]{1,0:T(4,128)S(1)}, f32[1,2304]{1,0:T(1,128)S(1)}, f32[1,2048]{1,0:T(1,128)S(1)}, f32[1,2048]{...) custom-call(bf16[1024,4384]{1,0:T(8,128)(2,1)} %convolution_convert_, ...), custom_call_target="tpu_custom_call", output_to_operand_aliasing={{1}: (14, {}), {2}: (15, {}), {3}: (16, {}), {4}: (17, {}),... | custom-call | flops 536870912 | bytes 5242880 | tf_op jit(solution)/shard_map/mix_backward/pallas_call | solution.py:408
  300.2 35.0 %mix_backward.5 = (bf16[1024,4384]{1,0:T(8,128)(2,1)}, f32[4,2304]{1,0:T(4,128)S(1)}, f32[1,2304]{1,0:T(1,128)S(1)}, f32[1,2048]{1,0:T(1,128)S(1)}, f32[1,2048]{...) custom-call(bf16[1024,4384]{1,0:T(8,128)(2,1)} %convolution_convert_, ...), custom_call_target="tpu_custom_call", output_to_operand_aliasing={{1}: (14, {}), {2}: (15, {}), {3}: (16, {}), {4}: (17, {}),... | custom-call | flops 536870912 | bytes 5242880 | tf_op jit(solution)/shard_map/mix_backward/pallas_call | solution.py:408
  353.0 6.7 convolution_convert_fusion.7
  376.7 17.5 %multiply_reduce_fusion = (f32[1024]{0:T(1024)S(1)}, f32[1024]{0:T(1024)S(1)}, f32[1024,1024]{1,0:T(8,128)}) fusion(f32[1024,1024]{1,0:T(8,128)} %get-tuple-element.320, f32[1024]{0:T(1024)S(1)} %copy-done.59, f32[1024]{0:T(1024)S(1)} %bitcast.201, bf16[1024,4384]{1,0:T(8,128)(2,1)} %get-tuple-element.159, ...), kind=kOutput, calls=%fused_computation.19 | convolution fusion | flops 9200203776 | bytes 26361856 | tf_op jit(solution)/shard_map/dot_general | solution.py:23
  394.2 7.4 %bitcast_add_fusion = f32[1024,1024]{1,0:T(8,128)} fusion(f32[2,512,1024]{2,1,0:T(8,128)} %param.14, f32[1024,1024]{1,0:T(8,128)} %get-tuple-element.321, f32[1024,1024]{1,0:T(8,128)} %get-tuple-element.320, f32[1024]{0:T(1024)S(1)} %broadcast_multiply_fusion.1, f32[1024]{0:T(1024)S(1)} %bitcast.202, f32[1024]{0:T(1024)S(1)} %copy-done.59), kind=kLoop, calls=%fused_computation.14 | loop fusion | flops 6291456 | bytes 16789504 | tf_op jit(solution)/shard_map/add | solution.py:783
  430.1 8.3 %convolution_convert_fusion.10.refs_5_ = bf16[1024,2048]{1,0:T(8,128)(2,1)} fusion(bf16[1024,1024]{1,0:T(8,128)(2,1)S(1)} %multiply_convert_fusion, bf16[2048,1024]{1,0:T(8,128)(2,1)} %assemble.1), kind=kOutput, calls=%fused_computation.40 | convolution fusion | flops 4297064448 | bytes 10485760 | tf_op jit(solution)/shard_map/dot_general | solution.py:23
  438.5 15.9 %collective-permute-done.15 = bf16[4,1,1,32,2176]{4,3,2,1,0:T(8,128)(2,1)S(1)} collective-permute-done((bf16[4,1,1,32,2176]{4,3,2,1,0:T(8,128)(2,1)}, bf16[4,1,1,32,2176]{4,3,2,1,0:T(8,128)(2,1)S(1)}, u32[]{:S(2)}, u32[]{:S(2)}) %collective-permute-start.15) | collective-permute-done | bytes 557088 | tf_op jit(solution)/shard_map/ppermute | solution.py:556
  470.0 35.1 %mix_backward.6 = (bf16[1024,4384]{1,0:T(8,128)(2,1)}, f32[4,2304]{1,0:T(4,128)S(1)}, f32[1,2304]{1,0:T(1,128)S(1)}, f32[1,2048]{1,0:T(1,128)S(1)}, f32[1,2048]{...) custom-call(bf16[1024,4384]{1,0:T(8,128)(2,1)} %convolution_convert_, ...), custom_call_target="tpu_custom_call", output_to_operand_aliasing={{1}: (14, {}), {2}: (15, {}), {3}: (16, {}), {4}: (17, {}),... | custom-call | flops 536870912 | bytes 5242880 | tf_op jit(solution)/shard_map/mix_backward/pallas_call | solution.py:408
  505.8 35.0 %mix_backward.7 = (bf16[1024,4384]{1,0:T(8,128)(2,1)}, f32[4,2304]{1,0:T(4,128)S(1)}, f32[1,2304]{1,0:T(1,128)S(1)}, f32[1,2048]{1,0:T(1,128)S(1)}, f32[1,2048]{...) custom-call(bf16[1024,4384]{1,0:T(8,128)(2,1)} %convolution_convert_, ...), custom_call_target="tpu_custom_call", output_to_operand_aliasing={{1}: (14, {}), {2}: (15, {}), {3}: (16, {}), {4}: (17, {}),... | custom-call | flops 536870912 | bytes 5242880 | tf_op jit(solution)/shard_map/mix_backward/pallas_call | solution.py:408
  540.9 6.5 convolution_convert_fusion.5
  553.8 6.7 convolution_convert_fusion.3
  579.5 16.6 %fusion.66 = f32[1024,1024]{1,0:T(8,128)} fusion(bf16[1024,4384]{1,0:T(8,128)(2,1)} %get-tuple-element.206, bf16[1024,4384]{1,0:T(8,128)(2,1)} %bitcast.215), kind=kOutput, calls=%fused_computation.217 | convolution fusion | flops 9193914368 | bytes 22151168 | tf_op jit(solution)/shard_map/dot_general | solution.py:23
  596.1 10.1 %collective-permute-done.25 = bf16[4,1,2,32,2176]{4,3,2,1,0:T(8,128)(2,1)} collective-permute-done((bf16[4,1,2,32,2176]{4,3,2,1,0:T(8,128)(2,1)}, bf16[4,1,2,32,2176]{4,3,2,1,0:T(8,128)(2,1)}, u32[]{:S(2)}, u32[]{:S(2)}) %collective-permute-start.25) | collective-permute-done | bytes 1114144 | tf_op jit(solution)/shard_map/ppermute | solution.py:556
  617.3 7.6 %collective-permute-done.27 = bf16[4,1,1,32,2176]{4,3,2,1,0:T(8,128)(2,1)S(1)} collective-permute-done((bf16[4,1,1,32,2176]{4,3,2,1,0:T(8,128)(2,1)S(1)}, bf16[4,1,1,32,2176]{4,3,2,1,0:T(8,128)(2,1)S(1)}, u32[]{:S(2)}, u32[]{:S(2)}) %collective-permute-start.27) | collective-permute-done | bytes 557088 | tf_op jit(solution)/shard_map/ppermute | solution.py:556
  653.9 11.3 %multiply_add_fusion.1 = f32[1024,1024]{1,0:T(8,128)} fusion(f32[1024,1024]{1,0:T(8,128)} %get-tuple-element.320, bf16[1024,2048]{1,0:T(8,128)(2,1)} %copy-done.4, bf16[2048,1024]{1,0:T(8,128)(2,1)} %all-gather.10.cloned.1.call-done, f32[1024]{0:T(1024)S(1)} %bitcast.208), kind=kOutput, calls=%fused_computation.27 | convolution fusion | flops 4297064448 | bytes 16781312 | tf_op jit(solution)/shard_map/dot_general | solution.py:23
  (419 shorter events, 266.0 us)
Async XLA Ops:
  7.2 102.6 %all-gather.20.cloned.1.call-start = ((), (), s32[]{:S(2)}) async-start(), calls=%async_computation.9 | async-start | bytes 9461760 | tf_op jit(solution)/shard_map/all_gather | solution.py:551
  13.9 178.1 %all-gather.22.cloned.1.call-start = ((), (), s32[]{:S(2)}) async-start(), calls=%async_computation.10 | async-start | bytes 9461760 | tf_op jit(solution)/shard_map/all_gather | solution.py:551
  15.5 240.1 %all-gather.10.cloned.1.call-start = ((), (), s32[]{:S(2)}) async-start(), calls=%async_computation.2 | async-start | bytes 4325376 | tf_op jit(solution)/shard_map/all_gather | solution.py:551
  165.8 171.0 %reduce-scatter.3.cloned.1.call-start = ((), (), s32[]{:S(2)}) async-start(), calls=%async_computation.3 | async-start | bytes 2228224 | tf_op jit(solution)/shard_map/reduce_scatter | solution.py:683
  255.6 155.6 %all-gather.12.cloned.1.call-start = ((), (), s32[]{:S(2)}) async-start(), calls=%async_computation.4 | async-start | bytes 1179648 | tf_op jit(solution)/shard_map/all_gather | solution.py:685
  353.0 187.9 %reduce-scatter.5.cloned.1.call-start = ((), (), s32[]{:S(2)}) async-start(), calls=%async_computation.5 | async-start | bytes 2228224 | tf_op jit(solution)/shard_map/reduce_scatter | solution.py:683
  376.1 26.9 %collective-permute-start.12 = (bf16[4,1,2,32,2176]{4,3,2,1,0:T(8,128)(2,1)}, bf16[4,1,2,32,2176]{4,3,2,1,0:T(8,128)(2,1)}, u32[]{:S(2)}, u32[]{:S(2)}) collective-permute-start(bf16[4,1,2,32,2176]{4,3,2,1,0:T(8,128)(2,1)} %constant_dynamic-slice_fusion.7), channel_id=1, source_target_pairs={{0,16},{8,24},{16,0},{24,8},{1,17},{9,25},{17,1},{25,9},{2,18},{10... | collective-permute-start | bytes 3342344 | tf_op jit(solution)/shard_map/ppermute | solution.py:556
  376.1 28.3 %collective-permute-start.13 = (bf16[4,2,1,32,2208]{4,3,2,1,0:T(8,128)(2,1)}, bf16[4,2,1,32,2208]{4,3,2,1,0:T(8,128)(2,1)}, u32[]{:S(2)}, u32[]{:S(2)}) collective-permute-start(bf16[4,2,1,32,2208]{4,3,2,1,0:T(8,128)(2,1)} %constant_dynamic-slice_fusion.6), channel_id=1, source_target_pairs={{0,8},{8,0},{16,24},{24,16},{1,9},{9,1},{17,25},{25,17},{2,10},{10... | collective-permute-start | bytes 3391496 | tf_op jit(solution)/shard_map/ppermute | solution.py:556
  425.7 263.0 %all-gather.16.cloned.1.call-start = ((), (), s32[]{:S(2)}) async-start(), calls=%async_computation.7 | async-start | bytes 2580480 | tf_op jit(solution)/shard_map/all_gather | solution.py:658
  428.0 26.4 %collective-permute-start.15 = (bf16[4,1,1,32,2176]{4,3,2,1,0:T(8,128)(2,1)}, bf16[4,1,1,32,2176]{4,3,2,1,0:T(8,128)(2,1)S(1)}, u32[]{:S(2)}, u32[]{:S(2)}) collective-permute-start(bf16[4,1,1,32,2176]{4,3,2,1,0:T(8,128)(2,1)} %constant_dynamic-slice_fusion.5), channel_id=1, source_target_pairs={{0,8},{8,0},{16,24},{24,16},{1,9},{9,1},{17,25},{25,17},{2,10},{10... | collective-permute-start | bytes 1671176 | tf_op jit(solution)/shard_map/ppermute | solution.py:556
  428.5 25.9 %collective-permute-start.16 = (bf16[4,1,1,32,2208]{4,3,2,1,0:T(8,128)(2,1)}, bf16[4,1,1,32,2208]{4,3,2,1,0:T(8,128)(2,1)S(1)}, u32[]{:S(2)}, u32[]{:S(2)}) collective-permute-start(bf16[4,1,1,32,2208]{4,3,2,1,0:T(8,128)(2,1)} %constant_dynamic-slice_fusion.4), channel_id=1, source_target_pairs={{0,16},{8,24},{16,0},{24,8},{1,17},{9,25},{17,1},{25,9},{2,18},{10... | collective-permute-start | bytes 1695752 | tf_op jit(solution)/shard_map/ppermute | solution.py:556
  460.0 45.1 %collective-permute-start.18 = (bf16[32,2176]{1,0:T(8,128)(2,1)}, bf16[32,2176]{1,0:T(8,128)(2,1)S(1)}, u32[]{:S(2)}, u32[]{:S(2)}) collective-permute-start(bf16[32,2176]{1,0:T(8,128)(2,1)} %get-tuple-element.181), channel_id=1, source_target_pairs={{0,2},{1,3},{2,0},{3,1},{4,6},{5,7},{6,4},{7,5},{8,10},{9,11},{10,... | collective-permute-start | bytes 417800 | tf_op jit(solution)/shard_map/ppermute | solution.py:561
  460.0 45.1 %collective-permute-start.19 = (bf16[32,2176]{1,0:T(8,128)(2,1)}, bf16[32,2176]{1,0:T(8,128)(2,1)S(1)}, u32[]{:S(2)}, u32[]{:S(2)}) collective-permute-start(bf16[32,2176]{1,0:T(8,128)(2,1)} %get-tuple-element.182), channel_id=1, source_target_pairs={{0,3},{1,0},{2,1},{3,2},{4,7},{5,4},{6,5},{7,6},{8,11},{9,8},{10,9... | collective-permute-start | bytes 417800 | tf_op jit(solution)/shard_map/ppermute | solution.py:561
  462.8 42.4 %collective-permute-start.20 = (bf16[32,2208]{1,0:T(8,128)(2,1)}, bf16[32,2208]{1,0:T(8,128)(2,1)S(1)}, u32[]{:S(2)}, u32[]{:S(2)}) collective-permute-start(bf16[32,2208]{1,0:T(8,128)(2,1)} %get-tuple-element.183), channel_id=1, source_target_pairs={{0,1},{1,2},{2,3},{3,0},{4,5},{5,6},{6,7},{7,4},{8,9},{9,10},{10,1... | collective-permute-start | bytes 423944 | tf_op jit(solution)/shard_map/ppermute | solution.py:561
  463.3 41.9 %collective-permute-start.21 = (bf16[32,2208]{1,0:T(8,128)(2,1)S(1)}, bf16[32,2208]{1,0:T(8,128)(2,1)S(1)}, u32[]{:S(2)}, u32[]{:S(2)}) collective-permute-start(bf16[32,2208]{1,0:T(8,128)(2,1)S(1)} %get-tuple-element.184), channel_id=1, source_target_pairs={{0,2},{1,3},{2,0},{3,1},{4,6},{5,7},{6,4},{7,5},{8,10},{9,11},{10,... | collective-permute-start | bytes 423944 | tf_op jit(solution)/shard_map/ppermute | solution.py:561
  466.6 38.6 %collective-permute-start.22 = (bf16[32,2208]{1,0:T(8,128)(2,1)S(1)}, bf16[32,2208]{1,0:T(8,128)(2,1)S(1)}, u32[]{:S(2)}, u32[]{:S(2)}) collective-permute-start(bf16[32,2208]{1,0:T(8,128)(2,1)S(1)} %get-tuple-element.185), channel_id=1, source_target_pairs={{0,3},{1,0},{2,1},{3,2},{4,7},{5,4},{6,5},{7,6},{8,11},{9,8},{10,9... | collective-permute-start | bytes 423944 | tf_op jit(solution)/shard_map/ppermute | solution.py:561
  505.1 127.1 %collective-permute-start.42 = (f32[120,128]{1,0:T(8,128)S(1)}, f32[120,128]{1,0:T(8,128)S(1)}, u32[]{:S(2)}, u32[]{:S(2)}) collective-permute-start(f32[120,128]{1,0:T(8,128)S(1)} %pad_bitcast_fusion), channel_id=1, source_target_pairs={{0,4},{4,0},{1,5},{5,1},{2,6},{6,2},{3,7},{7,3},{8,12},{12,8},{9,1... | collective-permute-start | bytes 184328 | tf_op jit(solution)/shard_map/ppermute | solution.py:561
  553.7 139.1 %all-gather.18.cloned.1.call-start = ((), (), s32[]{:S(2)}) async-start(), calls=%async_computation.8 | async-start | bytes 1179648 | tf_op jit(solution)/shard_map/all_gather | solution.py:685
  574.6 31.7 %collective-permute-start.25 = (bf16[4,1,2,32,2176]{4,3,2,1,0:T(8,128)(2,1)}, bf16[4,1,2,32,2176]{4,3,2,1,0:T(8,128)(2,1)}, u32[]{:S(2)}, u32[]{:S(2)}) collective-permute-start(bf16[4,1,2,32,2176]{4,3,2,1,0:T(8,128)(2,1)} %constant_dynamic-slice_fusion.3), channel_id=1, source_target_pairs={{0,16},{8,24},{16,0},{24,8},{1,17},{9,25},{17,1},{25,9},{2,18},{10... | collective-permute-start | bytes 3342344 | tf_op jit(solution)/shard_map/ppermute | solution.py:556
  579.5 28.1 %collective-permute-start.26 = (bf16[4,2,1,32,2208]{4,3,2,1,0:T(8,128)(2,1)S(1)}, bf16[4,2,1,32,2208]{4,3,2,1,0:T(8,128)(2,1)}, u32[]{:S(2)}, u32[]{:S(2)}) collective-permute-start(bf16[4,2,1,32,2208]{4,3,2,1,0:T(8,128)(2,1)S(1)} %constant_dynamic-slice_fusion.2), channel_id=1, source_target_pairs={{0,8},{8,0},{16,24},{24,16},{1,9},{9,1},{17,25},{25,17},{2,10},{10... | collective-permute-start | bytes 3391496 | tf_op jit(solution)/shard_map/ppermute | solution.py:556
  632.3 32.9 %collective-permute-start.44 = (f32[120,128]{1,0:T(8,128)S(1)}, f32[120,128]{1,0:T(8,128)S(1)}, u32[]{:S(2)}, u32[]{:S(2)}) collective-permute-start(f32[120,128]{1,0:T(8,128)S(1)} %fusion.58), channel_id=1, source_target_pairs={{0,16},{8,24},{16,0},{24,8},{1,17},{9,25},{17,1},{25,9},{2,18},{10... | collective-permute-start | bytes 184328 | tf_op jit(solution)/shard_map/ppermute | solution.py:561
  633.9 31.3 %collective-permute-start.45 = (f32[120,128]{1,0:T(8,128)S(1)}, f32[120,128]{1,0:T(8,128)S(1)}, u32[]{:S(2)}, u32[]{:S(2)}) collective-permute-start(f32[120,128]{1,0:T(8,128)S(1)} %fusion.58), channel_id=1, source_target_pairs={{0,24},{8,0},{16,8},{24,16},{1,25},{9,1},{17,9},{25,17},{2,26},{10... | collective-permute-start | bytes 184328 | tf_op jit(solution)/shard_map/ppermute | solution.py:561
  635.2 65.1 %all-gather.14.cloned.1.call-start = ((), (), s32[]{:S(2)}) async-start(), calls=%async_computation.6 | async-start | bytes 2580480 | tf_op jit(solution)/shard_map/all_gather | solution.py:658
  646.4 18.8 %collective-permute-start.43 = (f32[120,128]{1,0:T(8,128)S(1)}, f32[120,128]{1,0:T(8,128)S(1)}, u32[]{:S(2)}, u32[]{:S(2)}) collective-permute-start(f32[120,128]{1,0:T(8,128)S(1)} %fusion.58), channel_id=1, source_target_pairs={{0,8},{8,16},{16,24},{24,0},{1,9},{9,17},{17,25},{25,1},{2,10},{10... | collective-permute-start | bytes 184328 | tf_op jit(solution)/shard_map/ppermute | solution.py:561
  (106 other events, 2059.4 us)
Sparse Core Ops, SparseCore 0:
  14.0 95.7 all-gather.19
  112.7 79.3 all-gather.21
  194.9 60.6 all-gather.9
  257.7 78.9 reduce-scatter.2
  353.1 20.7 all-gather.11
  425.8 82.9 reduce-scatter.4
  553.8 31.4 all-gather.15
  635.3 20.8 all-gather.17
  658.1 30.5 all-gather.13
